TPU v7x, 128 devices: a whole 4x4x4 slice. The times are simulated.
128 devices in a mesh: span: 8 (over z, y_hi), chord: 16 (over y_lo, x, core).
Axes of the slice: x: 4, y: 4 (y_hi: 2, y_lo: 2; y = y_hi * 2 + y_lo), z: 4, core: 2. Of those that a mesh axis runs over, the one named last changes fastest.
Arguments:
- adjoint_next: float32 [5, 128, 512, 256], P(None, 'span', 'chord'), may hold values from -6 to 6
- objective_grad: bfloat16 [5, 128, 512, 256], P(None, 'span', 'chord'), may hold values from -6 to 6
- state_next: bfloat16 [8, 128, 512, 256], P(None, 'span', 'chord'), may hold values from -3 to 3, as said below
- checkpoint_pieces: bfloat16 [8, 16384, 1024], P(None, ('span', 'chord')), may hold values from -3 to 3, as said below
- slot_target: int32 [128, 128], P(('span', 'chord')), may hold values from 0 to 127, as said below
- piece_owner: int32 [128, 128], P(('span', 'chord')), may hold values from 0 to 127, as said below
- coupling: float32 [5, 5], replicated, may hold values from -1.5 to 1.5
Outputs:
- adjoint_field: float32 [5, 128, 512, 256], P(None, 'span', 'chord')
Inputs may be any that keep to these rules, and one draw needn't show every extreme that they name: `state_next`: fields 0 and 4 (density, energy) lie in [0.5, 2], fields 5 to 7 in [-1.5, 1.5]. `checkpoint_pieces`: fields 0 and 4 (density, energy) lie in [0.5, 2], fields 5 to 7 in [-1.5, 1.5]. `slot_target`: each row lists every device index once: an owner holds exactly one piece of every device's block. `piece_owner`: each row lists every owner once.
All inputs are finite; a program needn't handle non-finite values.
Results may differ from a plain program's by a relative error of at most 0.0003.
Values may be sent and summed in bfloat16 or wider, within the bound.
No kernel may reach another device: no remote copies, remote signals or barrier semaphores. Data moves between devices by JAX's collectives and lax.ppermute only.
A program may use at most 256 MiB of HBM per device.

v0:
```python
import functools

import jax
import jax.numpy as jnp
from jax import lax
from jax.experimental import pallas as pl
from jax.experimental.pallas import tpu as pltpu
from jax.sharding import PartitionSpec as P

NCONS = 5
NSTATE = 8
CS = 16
CC = 32
CN = 256
SWEEPS = 4
PIECE = 1024
TILES = CC // 8
LANES = 128
HALVES = CN // LANES
VELOCITY_CODE = 4368.0
ENERGY_CODE = 8190.0
MIB = 1 << 20


def in_vmem(array):
    return pltpu.with_memory_space_constraint(array, pltpu.VMEM)


def call(body, outs, args, scratch=(), name=None, smem=(), limit=24 * MIB, cost=4000000):
    specs = [
        pl.BlockSpec(memory_space=pltpu.SMEM if i in smem else pltpu.VMEM) for i in range(len(args))
    ]
    return pl.pallas_call(
        body,
        out_shape=[pltpu.VMEM(shape, dtype) for shape, dtype in outs],
        in_specs=specs,
        out_specs=[pl.BlockSpec(memory_space=pltpu.VMEM) for _ in outs],
        scratch_shapes=list(scratch),
        compiler_params=pltpu.CompilerParams(vmem_limit_bytes=limit),
        cost_estimate=pl.CostEstimate(flops=cost * 8, bytes_accessed=cost, transcendentals=0),
        name=name,
    )(*[a if i in smem else in_vmem(a) for i, a in enumerate(args)])


def lanes(half):
    return pl.ds(half * LANES, LANES)


def rows(tile):
    return pl.ds(tile * 8, 8)


def mask_of(shape_dim, value):
    return lax.broadcasted_iota(jnp.int32, (8, LANES), shape_dim) == value


class Field:
    def __init__(self, cells, span_low, span_high, chord_low, chord_high):
        self.cells = cells
        self.span_low = span_low
        self.span_high = span_high
        self.chord_low = chord_low
        self.chord_high = chord_high

    def center(self, m, s, t, h):
        return self.cells[m, s, rows(t), lanes(h)]

    def span(self, m, s, t, h, step, edge):
        if edge == step:
            source = self.span_high if step > 0 else self.span_low
            return source[m, rows(t), lanes(h)]
        return self.cells[m, s + step, rows(t), lanes(h)]

    def chord(self, m, s, t, h, step, center, first, last):
        if step > 0:
            if t == TILES - 1:
                beyond = jnp.broadcast_to(self.chord_high[s, pl.ds(m, 1), lanes(h)], (8, LANES))
            else:
                beyond = self.center(m, s, t + 1, h)
            return pltpu.roll(jnp.where(first, beyond, center), 7, 0)
        if t == 0:
            beyond = jnp.broadcast_to(self.chord_low[s, pl.ds(m, 1), lanes(h)], (8, LANES))
        else:
            beyond = self.center(m, s, t - 1, h)
        return pltpu.roll(jnp.where(last, beyond, center), 1, 0)


def normal(centers, h, step, lane_first, lane_last):
    if step > 0:
        source = jnp.where(lane_first, centers[h + 1], centers[h]) if h + 1 < HALVES else centers[h]
        return pltpu.roll(source, LANES - 1, 1)
    source = jnp.where(lane_last, centers[h - 1], centers[h]) if h > 0 else centers[h]
    return pltpu.roll(source, 1, 1)


def stencil(field, s, t, edge, factors, energies, bases, coupling):
    row_first, row_last = mask_of(0, 0), mask_of(0, 7)
    lane_first, lane_last = mask_of(1, 0), mask_of(1, LANES - 1)
    centers = [[field.center(m, s, t, h) for h in range(HALVES)] for m in range(NCONS)]
    out = []
    for m in range(NCONS):
        scalars = [coupling[n, m] for n in range(NCONS)]
        pair = []
        for h in range(HALVES):
            (span_up, span_low), (chord_up, chord_low), (normal_up, normal_low) = factors[h]
            mixed = scalars[0] * centers[0][h]
            for n in range(1, NCONS):
                mixed = mixed + scalars[n] * centers[n][h]
            total = bases(m, h, centers[m][h]) + energies[h] * mixed
            total = total + span_up * field.span(m, s, t, h, 1, edge)
            total = total + span_low * field.span(m, s, t, h, -1, edge)
            total = total + chord_up * field.chord(m, s, t, h, 1, centers[m][h], row_first, row_last)
            total = total + chord_low * field.chord(m, s, t, h, -1, centers[m][h], row_first, row_last)
            total = total + normal_up * normal(centers[m], h, 1, lane_first, lane_last)
            total = total + normal_low * normal(centers[m], h, -1, lane_first, lane_last)
            pair.append(total)
        out.append(pair)
    return out


def each_row(row):
    row(0, -1)

    def inner(s, carry):
        row(s, 0)
        return carry

    lax.fori_loop(1, CS - 1, inner, 0)
    row(CS - 1, 1)


def halves_of(velocity, h):
    pairs = []
    for a in range(3):
        up = jnp.maximum(-velocity[a], 0.0) + 0.25
        low = jnp.maximum(velocity[a], 0.0) + 0.25
        if a == 2 and h == HALVES - 1:
            up = jnp.where(mask_of(1, LANES - 1), 0.0, up)
        if a == 2 and h == 0:
            low = jnp.where(mask_of(1, 0), 0.0, low)
        pairs.append((up, low))
    return pairs


def write_edges(out, s, t, edge, span_low, span_high, chord_low, chord_high):
    for m in range(NCONS):
        for h in range(HALVES):
            tile = out[m][h]
            if edge == -1:
                span_low[m, rows(t), lanes(h)] = tile
            if edge == 1:
                span_high[m, rows(t), lanes(h)] = tile
            if t == 0:
                chord_low[s, pl.ds(m, 1), lanes(h)] = tile[0:1]
            if t == TILES - 1:
                chord_high[s, pl.ds(m, 1), lanes(h)] = tile[7:8]


def send_body(pieces, target, out, words):
    groups = pieces.shape[1] // 16

    def group(g, carry):
        for c in range(PIECE // LANES):
            read = lambda f: pieces[f, pl.ds(g * 16, 16), lanes(c)].astype(jnp.float32)
            ratio = 1.0 / read(0)
            codes = [jnp.round((read(1 + a) * ratio - read(5 + a)) * VELOCITY_CODE).astype(jnp.int32) for a in range(3)]
            codes.append(jnp.round(read(4) * ratio * ENERGY_CODE).astype(jnp.int32))
            for w in range(2):
                word = (codes[2 * w] << 16) | (codes[2 * w + 1] & 0xFFFF)
                for part in range(2):
                    words[w, pl.ds((g * 2 + part) * 64 + c * 8, 8), :] = word[part * 8 : part * 8 + 8]
        for j in range(16):
            d = target[0, g * 16 + j]
            for w in range(2):
                out[d, pl.ds(w * 8, 8), :] = words[w, pl.ds((g * 2 + j // 8) * 64 + j % 8, 8, stride=8), :]
        return carry

    lax.fori_loop(0, groups, group, 0)


def send_order(pieces, target):
    count = pieces.shape[1]
    return call(
        send_body,
        [((count, 16, LANES), jnp.int32)],
        [pieces, target],
        scratch=[pltpu.VMEM((2, count * 8, LANES), jnp.int32)],
        smem=(1,),
        name="send_order",
        cost=3 * MIB,
    )[0]


def right_body(v, state, grad, coupling, sl, sh, cl, ch, out):
    field = Field(v, sl, sh, cl, ch)

    def row(s, edge):
        for pair in range(TILES // 2):
            wide = lambda ref, f, h: ref[f, s, pl.ds(pair * 16, 16), lanes(h)].astype(jnp.float32)
            fields = [[wide(state, f, h) for h in range(HALVES)] for f in range(NSTATE)]
            gradient = [[wide(grad, m, h) for h in range(HALVES)] for m in range(NCONS)]
            for part in range(2):
                t = pair * 2 + part
                cut = lambda x: x[part * 8 : part * 8 + 8]
                factors, energies, middles = [], [], []
                for h in range(HALVES):
                    ratio = 1.0 / cut(fields[0][h])
                    velocity = [cut(fields[1 + a][h]) * ratio - cut(fields[5 + a][h]) for a in range(3)]
                    factors.append([(0.5 * up, 0.5 * low) for up, low in halves_of(velocity, h)])
                    energies.append(-0.5 * (cut(fields[4][h]) * ratio))
                    size = jnp.abs(velocity[0]) + jnp.abs(velocity[1]) + jnp.abs(velocity[2])
                    middles.append(0.25 - 0.5 * size)
                base = lambda m, h, center: cut(gradient[m][h]) + middles[h] * center
                result = stencil(field, s, t, edge, factors, energies, base, coupling)
                for m in range(NCONS):
                    for h in range(HALVES):
                        out[m, s, rows(t), lanes(h)] = result[m][h]

    each_row(row)


def first_body(v, words, owner, right, coupling, sl, sh, cl, ch, out, factor, scaled, el, eh, fl, fh, placed):
    field = Field(v, sl, sh, cl, ch)

    def place(k, carry):
        o = owner[0, k]
        for w in range(2):
            placed[w, pl.ds(pl.multiple_of(k * 8, 8), 8), :] = words[o, pl.ds(w * 8, 8), :]
        return carry

    lax.fori_loop(0, owner.shape[1], place, 0, unroll=8)

    def row(s, edge):
        for t in range(TILES):
            factors, energies, scales = [], [], []
            for h in range(HALVES):
                pair = [placed[w, pl.ds((s * 8 + t * 2) * 8 + h, 8, stride=2), :] for w in range(2)]
                codes = []
                for word in pair:
                    codes += [(word >> 16).astype(jnp.float32), ((word << 16) >> 16).astype(jnp.float32)]
                velocity = [codes[a] * (1.0 / VELOCITY_CODE) for a in range(3)]
                size = jnp.abs(velocity[0]) + jnp.abs(velocity[1]) + jnp.abs(velocity[2])
                scale = 1.0 / (1.75 + 0.5 * size)
                half = 0.5 * scale
                pairs = [(half * up, half * low) for up, low in halves_of(velocity, h)]
                energy = (-1.0 / ENERGY_CODE) * codes[3] * half
                factors.append(pairs)
                energies.append(energy)
                scales.append(scale)
                for a in range(3):
                    factor[2 * a, s, rows(t), lanes(h)] = pairs[a][0]
                    factor[2 * a + 1, s, rows(t), lanes(h)] = pairs[a][1]
                factor[6, s, rows(t), lanes(h)] = energy

            def base(m, h, center):
                value = right[m, s, rows(t), lanes(h)] * scales[h]
                scaled[m, s, rows(t), lanes(h)] = value
                return value

            result = stencil(field, s, t, edge, factors, energies, base, coupling)
            for m in range(NCONS):
                for h in range(HALVES):
                    out[m, s, rows(t), lanes(h)] = result[m][h]
            write_edges(result, s, t, edge, el, eh, fl, fh)

    each_row(row)


def sweep_body(edges, v, factor, scaled, coupling, sl, sh, cl, ch, out, *faces):
    field = Field(v, sl, sh, cl, ch)

    def row(s, edge):
        for t in range(TILES):
            read = lambda i, h: factor[i, s, rows(t), lanes(h)]
            factors = [[(read(2 * a, h), read(2 * a + 1, h)) for a in range(3)] for h in range(HALVES)]
            energies = [read(6, h) for h in range(HALVES)]
            base = lambda m, h, center: scaled[m, s, rows(t), lanes(h)]
            result = stencil(field, s, t, edge, factors, energies, base, coupling)
            for m in range(NCONS):
                for h in range(HALVES):
                    out[m, s, rows(t), lanes(h)] = result[m][h]
            if edges:
                write_edges(result, s, t, edge, *faces)

    each_row(row)


CELLS = ((NCONS, CS, CC, CN), jnp.float32)
FACES = [((NCONS, CC, CN), jnp.float32)] * 2 + [((CS, NCONS, CN), jnp.float32)] * 2


def exchange(faces):
    span_low, span_high, chord_low, chord_high = faces
    move = lambda x, axis, up: lax.ppermute(
        x,
        axis,
        [(i, i + 1) if up else (i + 1, i) for i in range(lax.axis_size(axis) - 1)],
    )
    return (
        move(span_high, "span", True),
        move(span_low, "span", False),
        move(chord_high, "chord", True),
        move(chord_low, "chord", False),
    )


def shards(adjoint_next, objective_grad, state_next, checkpoint_pieces, slot_target, piece_owner, coupling):
    outgoing = send_order(checkpoint_pieces, slot_target)
    incoming = lax.all_to_all(outgoing, ("span", "chord"), split_axis=0, concat_axis=0, tiled=True)
    halo = exchange(
        (
            adjoint_next[:, 0],
            adjoint_next[:, CS - 1],
            adjoint_next[:, :, 0].transpose(1, 0, 2),
            adjoint_next[:, :, CC - 1].transpose(1, 0, 2),
        )
    )
    right = call(
        right_body,
        [CELLS],
        [adjoint_next, state_next, objective_grad, coupling, *halo],
        smem=(3,),
        name="right_side",
        cost=9 * MIB,
    )[0]
    adjoint, factor, scaled, *faces = call(
        first_body,
        [CELLS, ((7, CS, CC, CN), jnp.float32), CELLS, *FACES],
        [adjoint_next, incoming, piece_owner, right, coupling, *halo],
        scratch=[pltpu.VMEM((2, 1024, LANES), jnp.int32)],
        smem=(2, 4),
        name="first_sweep",
        cost=9 * MIB,
    )
    for sweep in range(1, SWEEPS):
        more = sweep < SWEEPS - 1
        adjoint, *faces = call(
            functools.partial(sweep_body, more),
            [CELLS, *(FACES if more else [])],
            [adjoint, factor, scaled, coupling, *exchange(faces)],
            smem=(3,),
            name="sweep",
            cost=9 * MIB,
        )
    return adjoint


def solution(mesh):
    placed = (
        P(None, "span", "chord", None),
        P(None, "span", "chord", None),
        P(None, "span", "chord", None),
        P(None, ("span", "chord"), None),
        P(("span", "chord"), None),
        P(("span", "chord"), None),
        P(),
    )
    return jax.shard_map(
        shards,
        mesh=mesh,
        in_specs=placed,
        out_specs=P(None, "span", "chord", None),
        check_vma=False,
    )
```

profile of v0, /device:TPU:39, one launch (start us, length us, event | category | flops | bytes accessed | tf_op | source)
XLA Modules:
  0.0 121.0 jit_solution(12058707037987488597)
XLA Ops:
  4.6 10.9 %all-to-all-start = ((s32[128,16,128]{2,1,0:T(8,128)}), s32[128,16,128]{2,1,0:T(8,128)}, u32[]{:S(2)}, u32[]{:S(2)}) async-start(s32[128,16,128]{2,1,0:T(8,128)} %copy-done.3), calls=%async_computation | async-start | bytes 2097152 | tf_op jit(solution)/shard_map/all_to_all | solution.py:309
  15.6 4.5 %collective-permute-start.1 = (f32[5,32,256]{2,1,0:T(8,128)S(1)}, f32[5,32,256]{2,1,0:T(8,128)S(1)}, u32[]{:S(2)}, u32[]{:S(2)}) collective-permute-start(f32[5,32,256]{2,1,0:T(8,128)S(1)} %get-tuple-element.41), channel_id=1, source_target_pairs={{16,0},{32,16},{48,32},{64,48},{80,64},{96,80},{112,96},{17,1},{33... | collective-permute-start | bytes 491528 | tf_op jit(solution)/shard_map/ppermute | solution.py:294
  20.1 2.3 %collective-permute-start = (f32[5,32,256]{2,1,0:T(8,128)S(1)}, f32[5,32,256]{2,1,0:T(8,128)S(1)}, u32[]{:S(2)}, u32[]{:S(2)}) collective-permute-start(f32[5,32,256]{2,1,0:T(8,128)S(1)} %get-tuple-element.42), channel_id=1, source_target_pairs={{0,16},{16,32},{32,48},{48,64},{64,80},{80,96},{96,112},{1,17},{17... | collective-permute-start | bytes 491528 | tf_op jit(solution)/shard_map/ppermute | solution.py:294
  22.6 3.9 %collective-permute-start.2 = (f32[16,5,256]{2,1,0:T(8,128)S(1)}, f32[16,5,256]{2,1,0:T(8,128)S(1)}, u32[]{:S(2)}, u32[]{:S(2)}) collective-permute-start(f32[16,5,256]{2,1,0:T(8,128)S(1)} %bitcast.18), channel_id=1, source_target_pairs={{0,1},{1,2},{2,3},{3,4},{4,5},{5,6},{6,7},{7,8},{8,9},{9,10},{10,1... | collective-permute-start | bytes 245768 | tf_op jit(solution)/shard_map/ppermute | solution.py:294
  28.5 6.8 %collective-permute-done.3.ch = f32[16,5,256]{2,1,0:T(8,128)S(1)} collective-permute-done((f32[16,5,256]{2,1,0:T(8,128)S(1)}, f32[16,5,256]{2,1,0:T(8,128)S(1)}, u32[]{:S(2)}, u32[]{:S(2)}) %collective-permute-start.3) | collective-permute-done | bytes 81952 | tf_op jit(solution)/shard_map/ppermute | solution.py:294
  39.3 4.6 %right_side.1.right = f32[5,16,32,256]{3,2,1,0:T(8,128)S(1)} custom-call(f32[5,16,32,256]{3,2,1,0:T(8,128)S(1)} %copy-done, bf16[8,16,32,256]{3,2,1,0:T(8,128)(2,1)S(1)} %copy-done.5, bf16[5,16,32,256]{3,2,1,0:T(8,128)(2,1)S(1)} %copy-done.6, f32[5,5]{1,0:T(8,128)S(1)} %copy-done.7, f32[5,32,256]{2,1,0:T(8,128)S(1)} %collective-permute-done.sl, ...), custom_call_target="tpu_custom_call" | custom-call | flops 75497472 | bytes 9437184 | tf_op jit(solution)/shard_map/right_side/pallas_call | solution.py:33
  47.2 5.2 %first_sweep.1 = (f32[5,16,32,256]{3,2,1,0:T(8,128)S(1)}, f32[7,16,32,256]{3,2,1,0:T(8,128)S(1)}, f32[5,16,32,256]{3,2,1,0:T(8,128)S(1)}, f32[5,32,256]{2,1,0:T(...) custom-call(f32[5,16,32,256]{3,2,1,0:T(8,128)S(1)} %copy-done, ...), custom_call_target="tpu_custom_call" | custom-call | flops 75497472 | bytes 9437184 | tf_op jit(solution)/shard_map/first_sweep/pallas_call | solution.py:33
  52.4 4.0 %collective-permute-start.4 = (f32[5,32,256]{2,1,0:T(8,128)S(1)}, f32[5,32,256]{2,1,0:T(8,128)S(1)}, u32[]{:S(2)}, u32[]{:S(2)}) collective-permute-start(f32[5,32,256]{2,1,0:T(8,128)S(1)} %get-tuple-element.25), channel_id=1, source_target_pairs={{0,16},{16,32},{32,48},{48,64},{64,80},{80,96},{96,112},{1,17},{17... | collective-permute-start | bytes 491528 | tf_op jit(solution)/shard_map/ppermute | solution.py:294
  56.5 3.6 %collective-permute-start.5 = (f32[5,32,256]{2,1,0:T(8,128)S(1)}, f32[5,32,256]{2,1,0:T(8,128)S(1)}, u32[]{:S(2)}, u32[]{:S(2)}) collective-permute-start(f32[5,32,256]{2,1,0:T(8,128)S(1)} %get-tuple-element.26), channel_id=1, source_target_pairs={{16,0},{32,16},{48,32},{64,48},{80,64},{96,80},{112,96},{17,1},{33... | collective-permute-start | bytes 491528 | tf_op jit(solution)/shard_map/ppermute | solution.py:294
  60.1 3.2 %collective-permute-start.6 = (f32[16,5,256]{2,1,0:T(8,128)S(1)}, f32[16,5,256]{2,1,0:T(8,128)S(1)}, u32[]{:S(2)}, u32[]{:S(2)}) collective-permute-start(f32[16,5,256]{2,1,0:T(8,128)S(1)} %get-tuple-element.27), channel_id=1, source_target_pairs={{0,1},{1,2},{2,3},{3,4},{4,5},{5,6},{6,7},{7,8},{8,9},{9,10},{10,1... | collective-permute-start | bytes 245768 | tf_op jit(solution)/shard_map/ppermute | solution.py:294
  65.2 6.5 %collective-permute-done.7.ch = f32[16,5,256]{2,1,0:T(8,128)S(1)} collective-permute-done((f32[16,5,256]{2,1,0:T(8,128)S(1)}, f32[16,5,256]{2,1,0:T(8,128)S(1)}, u32[]{:S(2)}, u32[]{:S(2)}) %collective-permute-start.7) | collective-permute-done | bytes 81952 | tf_op jit(solution)/shard_map/ppermute | solution.py:294
  71.7 3.6 %sweep.3 = (f32[5,16,32,256]{3,2,1,0:T(8,128)S(1)}, f32[5,32,256]{2,1,0:T(8,128)S(1)}, f32[5,32,256]{2,1,0:T(8,128)S(1)}, f32[16,5,256]{2,1,0:T(8,128)S(1)}, f32[16,5,256]{2,1,0:T(8,128)S(1)}) custom-call(f32[5,16,32,256]{3,2,1,0:T(8,128)S(1)} %get-tuple-element.22.v, f32[7,16,32,256]{3,2,1,0:T(8,128)S(1)} %get-tuple-element.23.factor, ...), custom_call_target="tpu_custom_call" | custom-call | flops 75497472 | bytes 9437184 | tf_op jit(solution)/shard_map/sweep/pallas_call | solution.py:33
  75.3 2.9 %collective-permute-start.8 = (f32[5,32,256]{2,1,0:T(8,128)S(1)}, f32[5,32,256]{2,1,0:T(8,128)S(1)}, u32[]{:S(2)}, u32[]{:S(2)}) collective-permute-start(f32[5,32,256]{2,1,0:T(8,128)S(1)} %get-tuple-element.30), channel_id=1, source_target_pairs={{0,16},{16,32},{32,48},{48,64},{64,80},{80,96},{96,112},{1,17},{17... | collective-permute-start | bytes 491528 | tf_op jit(solution)/shard_map/ppermute | solution.py:294
  78.3 4.8 %collective-permute-start.9 = (f32[5,32,256]{2,1,0:T(8,128)S(1)}, f32[5,32,256]{2,1,0:T(8,128)S(1)}, u32[]{:S(2)}, u32[]{:S(2)}) collective-permute-start(f32[5,32,256]{2,1,0:T(8,128)S(1)} %get-tuple-element.31), channel_id=1, source_target_pairs={{16,0},{32,16},{48,32},{64,48},{80,64},{96,80},{112,96},{17,1},{33... | collective-permute-start | bytes 491528 | tf_op jit(solution)/shard_map/ppermute | solution.py:294
  83.0 2.3 %collective-permute-start.10 = (f32[16,5,256]{2,1,0:T(8,128)S(1)}, f32[16,5,256]{2,1,0:T(8,128)S(1)}, u32[]{:S(2)}, u32[]{:S(2)}) collective-permute-start(f32[16,5,256]{2,1,0:T(8,128)S(1)} %get-tuple-element.32), channel_id=1, source_target_pairs={{0,1},{1,2},{2,3},{3,4},{4,5},{5,6},{6,7},{7,8},{8,9},{9,10},{10,1... | collective-permute-start | bytes 245768 | tf_op jit(solution)/shard_map/ppermute | solution.py:294
  85.4 2.0 %collective-permute-start.11 = (f32[16,5,256]{2,1,0:T(8,128)S(1)}, f32[16,5,256]{2,1,0:T(8,128)S(1)}, u32[]{:S(2)}, u32[]{:S(2)}) collective-permute-start(f32[16,5,256]{2,1,0:T(8,128)S(1)} %get-tuple-element.33), channel_id=1, source_target_pairs={{1,0},{2,1},{3,2},{4,3},{5,4},{6,5},{7,6},{8,7},{9,8},{10,9},{11,1... | collective-permute-start | bytes 245768 | tf_op jit(solution)/shard_map/ppermute | solution.py:294
  87.4 6.4 %collective-permute-done.11.ch = f32[16,5,256]{2,1,0:T(8,128)S(1)} collective-permute-done((f32[16,5,256]{2,1,0:T(8,128)S(1)}, f32[16,5,256]{2,1,0:T(8,128)S(1)}, u32[]{:S(2)}, u32[]{:S(2)}) %collective-permute-start.11) | collective-permute-done | bytes 81952 | tf_op jit(solution)/shard_map/ppermute | solution.py:294
  93.8 3.6 %sweep.4 = (f32[5,16,32,256]{3,2,1,0:T(8,128)S(1)}, f32[5,32,256]{2,1,0:T(8,128)S(1)}, f32[5,32,256]{2,1,0:T(8,128)S(1)}, f32[16,5,256]{2,1,0:T(8,128)S(1)}, f32[16,5,256]{2,1,0:T(8,128)S(1)}) custom-call(f32[5,16,32,256]{3,2,1,0:T(8,128)S(1)} %get-tuple-element.29.v, f32[7,16,32,256]{3,2,1,0:T(8,128)S(1)} %get-tuple-element.23.factor, ...), custom_call_target="tpu_custom_call" | custom-call | flops 75497472 | bytes 9437184 | tf_op jit(solution)/shard_map/sweep/pallas_call | solution.py:33
  97.4 2.5 %collective-permute-start.12 = (f32[5,32,256]{2,1,0:T(8,128)S(1)}, f32[5,32,256]{2,1,0:T(8,128)S(1)}, u32[]{:S(2)}, u32[]{:S(2)}) collective-permute-start(f32[5,32,256]{2,1,0:T(8,128)S(1)} %get-tuple-element.35), channel_id=1, source_target_pairs={{0,16},{16,32},{32,48},{48,64},{64,80},{80,96},{96,112},{1,17},{17... | collective-permute-start | bytes 491528 | tf_op jit(solution)/shard_map/ppermute | solution.py:294
  100.0 5.2 %collective-permute-start.13 = (f32[5,32,256]{2,1,0:T(8,128)S(1)}, f32[5,32,256]{2,1,0:T(8,128)S(1)}, u32[]{:S(2)}, u32[]{:S(2)}) collective-permute-start(f32[5,32,256]{2,1,0:T(8,128)S(1)} %get-tuple-element.36), channel_id=1, source_target_pairs={{16,0},{32,16},{48,32},{64,48},{80,64},{96,80},{112,96},{17,1},{33... | collective-permute-start | bytes 491528 | tf_op jit(solution)/shard_map/ppermute | solution.py:294
  105.2 2.3 %collective-permute-start.14 = (f32[16,5,256]{2,1,0:T(8,128)S(1)}, f32[16,5,256]{2,1,0:T(8,128)S(1)}, u32[]{:S(2)}, u32[]{:S(2)}) collective-permute-start(f32[16,5,256]{2,1,0:T(8,128)S(1)} %get-tuple-element.37), channel_id=1, source_target_pairs={{0,1},{1,2},{2,3},{3,4},{4,5},{5,6},{6,7},{7,8},{8,9},{9,10},{10,1... | collective-permute-start | bytes 245768 | tf_op jit(solution)/shard_map/ppermute | solution.py:294
  107.5 2.0 %collective-permute-start.15 = (f32[16,5,256]{2,1,0:T(8,128)S(1)}, f32[16,5,256]{2,1,0:T(8,128)S(1)}, u32[]{:S(2)}, u32[]{:S(2)}) collective-permute-start(f32[16,5,256]{2,1,0:T(8,128)S(1)} %get-tuple-element.38), channel_id=1, source_target_pairs={{1,0},{2,1},{3,2},{4,3},{5,4},{6,5},{7,6},{8,7},{9,8},{10,9},{11,1... | collective-permute-start | bytes 245768 | tf_op jit(solution)/shard_map/ppermute | solution.py:294
  109.5 6.4 %collective-permute-done.15.ch = f32[16,5,256]{2,1,0:T(8,128)S(1)} collective-permute-done((f32[16,5,256]{2,1,0:T(8,128)S(1)}, f32[16,5,256]{2,1,0:T(8,128)S(1)}, u32[]{:S(2)}, u32[]{:S(2)}) %collective-permute-start.15) | collective-permute-done | bytes 81952 | tf_op jit(solution)/shard_map/ppermute | solution.py:294
  115.9 3.6 %sweep.5 = f32[5,16,32,256]{3,2,1,0:T(8,128)S(1)} custom-call(f32[5,16,32,256]{3,2,1,0:T(8,128)S(1)} %get-tuple-element.34.v, f32[7,16,32,256]{3,2,1,0:T(8,128)S(1)} %get-tuple-element.23.factor, f32[5,16,32,256]{3,2,1,0:T(8,128)S(1)} %get-tuple-element.24.scaled, f32[5,5]{1,0:T(8,128)S(1)} %copy-done.7, f32[5,32,256]{2,1,0:T(8,128)S(1)} %collective-permute-done.12.sl, ...), custom_call_target="tpu_custom_call" | custom-call | flops 75497472 | bytes 9437184 | tf_op jit(solution)/shard_map/sweep/pallas_call | solution.py:33
  (41 shorter events, 17.4 us)
Async XLA Ops:
  0.0 15.5 %copy-start = (f32[5,16,32,256]{3,2,1,0:T(8,128)S(1)}, f32[5,16,32,256]{3,2,1,0:T(8,128)}, u32[]{:S(2)}) copy-start(f32[5,16,32,256]{3,2,1,0:T(8,128)} %v.3) | copy-start | bytes 7864324
  0.0 1.7 %copy-start.4 = (bf16[8,128,1024]{2,1,0:T(8,128)(2,1)S(1)}, bf16[8,128,1024]{2,1,0:T(8,128)(2,1)}, u32[]{:S(2)}) copy-start(bf16[8,128,1024]{2,1,0:T(8,128)(2,1)} %pieces.1) | copy-start | bytes 6291460
  2.4 34.0 %copy-start.7 = (f32[5,5]{1,0:T(8,128)S(1)}, f32[5,5]{1,0:T(8,128)}, u32[]{:S(2)}) copy-start(f32[5,5]{1,0:T(8,128)} %coupling.9) | copy-start | bytes 304
  4.6 40.9 %all-to-all-start = ((s32[128,16,128]{2,1,0:T(8,128)}), s32[128,16,128]{2,1,0:T(8,128)}, u32[]{:S(2)}, u32[]{:S(2)}) async-start(s32[128,16,128]{2,1,0:T(8,128)} %copy-done.3), calls=%async_computation | async-start | bytes 2097152 | tf_op jit(solution)/shard_map/all_to_all | solution.py:309
  15.6 19.7 %collective-permute-start.1 = (f32[5,32,256]{2,1,0:T(8,128)S(1)}, f32[5,32,256]{2,1,0:T(8,128)S(1)}, u32[]{:S(2)}, u32[]{:S(2)}) collective-permute-start(f32[5,32,256]{2,1,0:T(8,128)S(1)} %get-tuple-element.41), channel_id=1, source_target_pairs={{16,0},{32,16},{48,32},{64,48},{80,64},{96,80},{112,96},{17,1},{33... | collective-permute-start | bytes 491528 | tf_op jit(solution)/shard_map/ppermute | solution.py:294
  20.1 16.3 %collective-permute-start = (f32[5,32,256]{2,1,0:T(8,128)S(1)}, f32[5,32,256]{2,1,0:T(8,128)S(1)}, u32[]{:S(2)}, u32[]{:S(2)}) collective-permute-start(f32[5,32,256]{2,1,0:T(8,128)S(1)} %get-tuple-element.42), channel_id=1, source_target_pairs={{0,16},{16,32},{32,48},{48,64},{64,80},{80,96},{96,112},{1,17},{17... | collective-permute-start | bytes 491528 | tf_op jit(solution)/shard_map/ppermute | solution.py:294
  22.6 6.0 %collective-permute-start.2 = (f32[16,5,256]{2,1,0:T(8,128)S(1)}, f32[16,5,256]{2,1,0:T(8,128)S(1)}, u32[]{:S(2)}, u32[]{:S(2)}) collective-permute-start(f32[16,5,256]{2,1,0:T(8,128)S(1)} %bitcast.18), channel_id=1, source_target_pairs={{0,1},{1,2},{2,3},{3,4},{4,5},{5,6},{6,7},{7,8},{8,9},{9,10},{10,1... | collective-permute-start | bytes 245768 | tf_op jit(solution)/shard_map/ppermute | solution.py:294
  26.6 18.9 %copy-start.8 = (s32[1,128]{1,0:T(1,128)S(1)}, s32[1,128]{1,0:T(1,128)}, u32[]{:S(2)}) copy-start(s32[1,128]{1,0:T(1,128)} %owner.1) | copy-start | bytes 1540
  26.6 8.7 %collective-permute-start.3 = (f32[16,5,256]{2,1,0:T(8,128)S(1)}, f32[16,5,256]{2,1,0:T(8,128)S(1)}, u32[]{:S(2)}, u32[]{:S(2)}) collective-permute-start(f32[16,5,256]{2,1,0:T(8,128)S(1)} %bitcast.19), channel_id=1, source_target_pairs={{1,0},{2,1},{3,2},{4,3},{5,4},{6,5},{7,6},{8,7},{9,8},{10,9},{11,1... | collective-permute-start | bytes 245768 | tf_op jit(solution)/shard_map/ppermute | solution.py:294
  36.4 1.6 %copy-start.5 = (bf16[8,16,32,256]{3,2,1,0:T(8,128)(2,1)S(1)}, bf16[8,16,32,256]{3,2,1,0:T(8,128)(2,1)}, u32[]{:S(2)}) copy-start(bf16[8,16,32,256]{3,2,1,0:T(8,128)(2,1)} %state.1) | copy-start | bytes 6291460
  44.0 1.5 %copy-start.1 = (f32[5,16,32,256]{3,2,1,0:T(8,128)}, f32[5,16,32,256]{3,2,1,0:T(8,128)S(1)}, u32[]{:S(2)}) copy-start(f32[5,16,32,256]{3,2,1,0:T(8,128)S(1)} %right_side.1.right) | copy-start | bytes 7864324
  45.5 1.7 %copy-start.2 = (f32[5,16,32,256]{3,2,1,0:T(8,128)S(1)}, f32[5,16,32,256]{3,2,1,0:T(8,128)}, u32[]{:S(2)}) copy-start(f32[5,16,32,256]{3,2,1,0:T(8,128)} %copy-done.1) | copy-start | bytes 7864324
  52.4 19.3 %collective-permute-start.4 = (f32[5,32,256]{2,1,0:T(8,128)S(1)}, f32[5,32,256]{2,1,0:T(8,128)S(1)}, u32[]{:S(2)}, u32[]{:S(2)}) collective-permute-start(f32[5,32,256]{2,1,0:T(8,128)S(1)} %get-tuple-element.25), channel_id=1, source_target_pairs={{0,16},{16,32},{32,48},{48,64},{64,80},{80,96},{96,112},{1,17},{17... | collective-permute-start | bytes 491528 | tf_op jit(solution)/shard_map/ppermute | solution.py:294
  56.5 15.2 %collective-permute-start.5 = (f32[5,32,256]{2,1,0:T(8,128)S(1)}, f32[5,32,256]{2,1,0:T(8,128)S(1)}, u32[]{:S(2)}, u32[]{:S(2)}) collective-permute-start(f32[5,32,256]{2,1,0:T(8,128)S(1)} %get-tuple-element.26), channel_id=1, source_target_pairs={{16,0},{32,16},{48,32},{64,48},{80,64},{96,80},{112,96},{17,1},{33... | collective-permute-start | bytes 491528 | tf_op jit(solution)/shard_map/ppermute | solution.py:294
  60.1 5.1 %collective-permute-start.6 = (f32[16,5,256]{2,1,0:T(8,128)S(1)}, f32[16,5,256]{2,1,0:T(8,128)S(1)}, u32[]{:S(2)}, u32[]{:S(2)}) collective-permute-start(f32[16,5,256]{2,1,0:T(8,128)S(1)} %get-tuple-element.27), channel_id=1, source_target_pairs={{0,1},{1,2},{2,3},{3,4},{4,5},{5,6},{6,7},{7,8},{8,9},{9,10},{10,1... | collective-permute-start | bytes 245768 | tf_op jit(solution)/shard_map/ppermute | solution.py:294
  63.3 8.4 %collective-permute-start.7 = (f32[16,5,256]{2,1,0:T(8,128)S(1)}, f32[16,5,256]{2,1,0:T(8,128)S(1)}, u32[]{:S(2)}, u32[]{:S(2)}) collective-permute-start(f32[16,5,256]{2,1,0:T(8,128)S(1)} %get-tuple-element.28), channel_id=1, source_target_pairs={{1,0},{2,1},{3,2},{4,3},{5,4},{6,5},{7,6},{8,7},{9,8},{10,9},{11,1... | collective-permute-start | bytes 245768 | tf_op jit(solution)/shard_map/ppermute | solution.py:294
  75.3 18.5 %collective-permute-start.8 = (f32[5,32,256]{2,1,0:T(8,128)S(1)}, f32[5,32,256]{2,1,0:T(8,128)S(1)}, u32[]{:S(2)}, u32[]{:S(2)}) collective-permute-start(f32[5,32,256]{2,1,0:T(8,128)S(1)} %get-tuple-element.30), channel_id=1, source_target_pairs={{0,16},{16,32},{32,48},{48,64},{64,80},{80,96},{96,112},{1,17},{17... | collective-permute-start | bytes 491528 | tf_op jit(solution)/shard_map/ppermute | solution.py:294
  78.3 15.5 %collective-permute-start.9 = (f32[5,32,256]{2,1,0:T(8,128)S(1)}, f32[5,32,256]{2,1,0:T(8,128)S(1)}, u32[]{:S(2)}, u32[]{:S(2)}) collective-permute-start(f32[5,32,256]{2,1,0:T(8,128)S(1)} %get-tuple-element.31), channel_id=1, source_target_pairs={{16,0},{32,16},{48,32},{64,48},{80,64},{96,80},{112,96},{17,1},{33... | collective-permute-start | bytes 491528 | tf_op jit(solution)/shard_map/ppermute | solution.py:294
  83.0 4.3 %collective-permute-start.10 = (f32[16,5,256]{2,1,0:T(8,128)S(1)}, f32[16,5,256]{2,1,0:T(8,128)S(1)}, u32[]{:S(2)}, u32[]{:S(2)}) collective-permute-start(f32[16,5,256]{2,1,0:T(8,128)S(1)} %get-tuple-element.32), channel_id=1, source_target_pairs={{0,1},{1,2},{2,3},{3,4},{4,5},{5,6},{6,7},{7,8},{8,9},{9,10},{10,1... | collective-permute-start | bytes 245768 | tf_op jit(solution)/shard_map/ppermute | solution.py:294
  85.4 8.4 %collective-permute-start.11 = (f32[16,5,256]{2,1,0:T(8,128)S(1)}, f32[16,5,256]{2,1,0:T(8,128)S(1)}, u32[]{:S(2)}, u32[]{:S(2)}) collective-permute-start(f32[16,5,256]{2,1,0:T(8,128)S(1)} %get-tuple-element.33), channel_id=1, source_target_pairs={{1,0},{2,1},{3,2},{4,3},{5,4},{6,5},{7,6},{8,7},{9,8},{10,9},{11,1... | collective-permute-start | bytes 245768 | tf_op jit(solution)/shard_map/ppermute | solution.py:294
  97.4 18.5 %collective-permute-start.12 = (f32[5,32,256]{2,1,0:T(8,128)S(1)}, f32[5,32,256]{2,1,0:T(8,128)S(1)}, u32[]{:S(2)}, u32[]{:S(2)}) collective-permute-start(f32[5,32,256]{2,1,0:T(8,128)S(1)} %get-tuple-element.35), channel_id=1, source_target_pairs={{0,16},{16,32},{32,48},{48,64},{64,80},{80,96},{96,112},{1,17},{17... | collective-permute-start | bytes 491528 | tf_op jit(solution)/shard_map/ppermute | solution.py:294
  100.0 15.9 %collective-permute-start.13 = (f32[5,32,256]{2,1,0:T(8,128)S(1)}, f32[5,32,256]{2,1,0:T(8,128)S(1)}, u32[]{:S(2)}, u32[]{:S(2)}) collective-permute-start(f32[5,32,256]{2,1,0:T(8,128)S(1)} %get-tuple-element.36), channel_id=1, source_target_pairs={{16,0},{32,16},{48,32},{64,48},{80,64},{96,80},{112,96},{17,1},{33... | collective-permute-start | bytes 491528 | tf_op jit(solution)/shard_map/ppermute | solution.py:294
  105.2 4.3 %collective-permute-start.14 = (f32[16,5,256]{2,1,0:T(8,128)S(1)}, f32[16,5,256]{2,1,0:T(8,128)S(1)}, u32[]{:S(2)}, u32[]{:S(2)}) collective-permute-start(f32[16,5,256]{2,1,0:T(8,128)S(1)} %get-tuple-element.37), channel_id=1, source_target_pairs={{0,1},{1,2},{2,3},{3,4},{4,5},{5,6},{6,7},{7,8},{8,9},{9,10},{10,1... | collective-permute-start | bytes 245768 | tf_op jit(solution)/shard_map/ppermute | solution.py:294
  107.5 8.4 %collective-permute-start.15 = (f32[16,5,256]{2,1,0:T(8,128)S(1)}, f32[16,5,256]{2,1,0:T(8,128)S(1)}, u32[]{:S(2)}, u32[]{:S(2)}) collective-permute-start(f32[16,5,256]{2,1,0:T(8,128)S(1)} %get-tuple-element.38), channel_id=1, source_target_pairs={{1,0},{2,1},{3,2},{4,3},{5,4},{6,5},{7,6},{8,7},{9,8},{10,9},{11,1... | collective-permute-start | bytes 245768 | tf_op jit(solution)/shard_map/ppermute | solution.py:294
  (3 other events, 2.9 us)
where the time goes:
time: 122 us; the launch traced here: 121 us
  starting transfers between devices  60.4 us (50%)
  waiting for transfers between devices  27.1 us (22%)
  Pallas kernels  22 us (18%)
  local copies, waits for them, and re-layouts  11.3 us (9%)
    ppermute x16, starting transfers between devices, exchange(): lax.ppermute(x, axis, [(i, i + 1) if up else (i + 1, i) for i in range(la...  49.4 us
    ppermute x16, waiting for transfers between devices, exchange(): lax.ppermute(x, axis, [(i, i + 1) if up else (i + 1, i) for i in range(la...  27.1 us
    pallas_call x6, Pallas kernels, call(): pl.pallas_call(body, out_shape=[pltpu.VMEM(shape, dtype) for shape, dtype...  22 us
    unnamed x23, local copies, waits for them, and re-layouts  11.1 us
    all_to_all x1, starting transfers between devices, shards(): lax.all_to_all(outgoing, ('span', 'chord'), split_axis=0, concat_axis=0,...  10.9 us
  transfers between devices with their start and end apart: 17, of which 5 were waited for; matrix products, arithmetic and copies ran while one was open for 0% of the time, Pallas kernels for 4%

commit v1 on v0

v1 whole, which is shorter than its diff:
```python
import jax
import jax.numpy as jnp
from jax import lax
from jax.experimental import pallas as pl
from jax.experimental.pallas import tpu as pltpu
from jax.sharding import PartitionSpec as P

NCONS = 5
NSTATE = 8
CS = 16
CC = 32
CN = 256
SWEEPS = 4
PIECE = 1024
TILES = CC // 8
LANES = 128
HALVES = CN // LANES
VELOCITY_CODE = 4368.0
ENERGY_CODE = 8190.0
MIB = 1 << 20
F32 = jnp.float32
BF16 = jnp.bfloat16


def in_space(array, space):
    return pltpu.with_memory_space_constraint(array, space)


def call(body, outs, args, scratch=(), name=None, smem=(), hbm=(), hbm_outs=(), limit=24 * MIB, cost=4 * MIB):
    space = lambda i: pltpu.SMEM if i in smem else pltpu.HBM if i in hbm else pltpu.VMEM
    out_space = lambda i: pltpu.HBM if i in hbm_outs else pltpu.VMEM
    return pl.pallas_call(
        body,
        out_shape=[out_space(i)(shape, dtype) for i, (shape, dtype) in enumerate(outs)],
        in_specs=[pl.BlockSpec(memory_space=space(i)) for i in range(len(args))],
        out_specs=[pl.BlockSpec(memory_space=out_space(i)) for i in range(len(outs))],
        scratch_shapes=list(scratch),
        compiler_params=pltpu.CompilerParams(vmem_limit_bytes=limit),
        cost_estimate=pl.CostEstimate(flops=cost * 8, bytes_accessed=cost, transcendentals=0),
        name=name,
    )(*[a if i in smem else in_space(a, space(i)) for i, a in enumerate(args)])


def lanes(half):
    return pl.ds(half * LANES, LANES)


def rows(tile):
    return pl.ds(tile * 8, 8)


def wide_rows(pair):
    return pl.ds(pair * 16, 16)


def mask_of(dim, value):
    return lax.broadcasted_iota(jnp.int32, (8, LANES), dim) == value


SPAN_FACE = ((NCONS, CC, CN), BF16)
CHORD_FACE = ((CS // 2, 16, CN), BF16)
FACES = [SPAN_FACE, SPAN_FACE, CHORD_FACE, CHORD_FACE]
SPAN_HALO = pltpu.VMEM((2, NCONS, CC, CN), F32)
CHORD_HALO = pltpu.VMEM((2, CS, 8, CN), F32)


def parity(axis):
    return lax.rem(lax.axis_index(axis), 2)


def unpack_faces(faces, span_halo, chord_halo):
    span_a, span_b, chord_a, chord_b = faces
    p = parity("span")
    for face, side in ((span_a, 1 - p), (span_b, p)):
        for m in range(NCONS):
            for pair in range(CC // 16):
                span_halo[side, m, wide_rows(pair), :] = face[m, wide_rows(pair), :].astype(F32)
    p = parity("chord")
    for face, side in ((chord_a, 1 - p), (chord_b, p)):
        for group in range(CS // 2):
            both = face[group].astype(F32)
            chord_halo[side, 2 * group] = both[:8]
            chord_halo[side, 2 * group + 1] = both[8:]


def pack_faces(cells, chord_edge, faces):
    span_a, span_b, chord_a, chord_b = faces
    p = parity("span")
    for face, side in ((span_a, 1 - p), (span_b, p)):
        for m in range(NCONS):
            for pair in range(CC // 16):
                face[m, wide_rows(pair), :] = cells[m, side * (CS - 1), wide_rows(pair), :].astype(BF16)
    p = parity("chord")
    for face, side in ((chord_a, 1 - p), (chord_b, p)):
        for group in range(CS // 2):
            both = [chord_edge[side, 2 * group], chord_edge[side, 2 * group + 1]]
            face[group] = jnp.concatenate(both, axis=0).astype(BF16)


def clear_padding(chord_edge):
    for side in range(2):
        for s in range(CS):
            chord_edge[side, s] = jnp.zeros((8, CN), F32)


def faces_body(cells, span_a, span_b, chord_a, chord_b, chord_edge):
    clear_padding(chord_edge)
    for s in range(CS):
        for m in range(NCONS):
            chord_edge[0, s, pl.ds(m, 1), :] = cells[m, s, pl.ds(0, 1), :]
            chord_edge[1, s, pl.ds(m, 1), :] = cells[m, s, pl.ds(CC - 1, 1), :]
    pack_faces(cells, chord_edge, (span_a, span_b, chord_a, chord_b))


def exchange(faces):
    def swap(face, axis, start):
        count = lax.axis_size(axis)
        pairs = [(i, i + 1) for i in range(start, count - 1, 2)]
        return lax.ppermute(face, axis, pairs + [(b, a) for a, b in pairs])

    span_a, span_b, chord_a, chord_b = faces
    return swap(span_a, "span", 0), swap(span_b, "span", 1), swap(chord_a, "chord", 0), swap(chord_b, "chord", 1)


class Field:
    def __init__(self, cells, span_halo, chord_halo):
        self.cells = cells
        self.span_halo = span_halo
        self.chord_halo = chord_halo

    def center(self, m, s, t, h):
        return self.cells[m, s, rows(t), lanes(h)]

    def span(self, m, s, t, h, step, edge):
        if edge == step:
            return self.span_halo[1 if step > 0 else 0, m, rows(t), lanes(h)]
        return self.cells[m, s + step, rows(t), lanes(h)]

    def beyond(self, side, m, s, h):
        return jnp.broadcast_to(self.chord_halo[side, s, pl.ds(m, 1), lanes(h)], (8, LANES))

    def chord(self, m, s, t, h, step, center, first, last):
        if step > 0:
            after = self.beyond(1, m, s, h) if t == TILES - 1 else self.center(m, s, t + 1, h)
            return pltpu.roll(jnp.where(first, after, center), 7, 0)
        before = self.beyond(0, m, s, h) if t == 0 else self.center(m, s, t - 1, h)
        return pltpu.roll(jnp.where(last, before, center), 1, 0)


def normal(centers, h, step, lane_first, lane_last):
    if step > 0:
        source = jnp.where(lane_first, centers[h + 1], centers[h]) if h + 1 < HALVES else centers[h]
        return pltpu.roll(source, LANES - 1, 1)
    source = jnp.where(lane_last, centers[h - 1], centers[h]) if h > 0 else centers[h]
    return pltpu.roll(source, 1, 1)


def stencil(field, s, t, edge, factors, energies, bases, coupling):
    row_first, row_last = mask_of(0, 0), mask_of(0, 7)
    lane_first, lane_last = mask_of(1, 0), mask_of(1, LANES - 1)
    centers = [[field.center(m, s, t, h) for h in range(HALVES)] for m in range(NCONS)]
    out = []
    for m in range(NCONS):
        scalars = [coupling[n, m] for n in range(NCONS)]
        pair = []
        for h in range(HALVES):
            (span_up, span_low), (chord_up, chord_low), (normal_up, normal_low) = factors[h]
            mixed = scalars[0] * centers[0][h]
            for n in range(1, NCONS):
                mixed = mixed + scalars[n] * centers[n][h]
            total = bases(m, h, centers[m][h]) + energies[h] * mixed
            total = total + span_up * field.span(m, s, t, h, 1, edge)
            total = total + span_low * field.span(m, s, t, h, -1, edge)
            total = total + chord_up * field.chord(m, s, t, h, 1, centers[m][h], row_first, row_last)
            total = total + chord_low * field.chord(m, s, t, h, -1, centers[m][h], row_first, row_last)
            total = total + normal_up * normal(centers[m], h, 1, lane_first, lane_last)
            total = total + normal_low * normal(centers[m], h, -1, lane_first, lane_last)
            pair.append(total)
        out.append(pair)
    return out


def each_row(row):
    row(0, -1)

    def inner(s, carry):
        row(s, 0)
        return carry

    lax.fori_loop(1, CS - 1, inner, 0)
    row(CS - 1, 1)


def halves_of(velocity, h):
    pairs = []
    for a in range(3):
        up = jnp.maximum(-velocity[a], 0.0) + 0.25
        low = jnp.maximum(velocity[a], 0.0) + 0.25
        if a == 2 and h == HALVES - 1:
            up = jnp.where(mask_of(1, LANES - 1), 0.0, up)
        if a == 2 and h == 0:
            low = jnp.where(mask_of(1, 0), 0.0, low)
        pairs.append((up, low))
    return pairs


def put(out, result, s, t, chord_edge=None):
    for m in range(NCONS):
        for h in range(HALVES):
            tile = result[m][h]
            out[m, s, rows(t), lanes(h)] = tile
            if chord_edge is not None and t == 0:
                chord_edge[0, s, pl.ds(m, 1), lanes(h)] = tile[0:1]
            if chord_edge is not None and t == TILES - 1:
                chord_edge[1, s, pl.ds(m, 1), lanes(h)] = tile[7:8]


SLOTS = 16


def send_body(pieces, target, out, taken, words, ordered, in_sem, out_sem):
    groups = pieces.shape[1] // SLOTS
    take = lambda g: pltpu.make_async_copy(
        pieces.at[:, pl.ds(g * SLOTS, SLOTS)], taken.at[:, pl.ds(g * SLOTS, SLOTS)], in_sem.at[g]
    )
    for g in range(groups):
        take(g).start()

    def group(g, carry):
        take(g).wait()
        for c in range(PIECE // LANES):
            read = lambda f: taken[f, pl.ds(pl.multiple_of(g * SLOTS, SLOTS), SLOTS), lanes(c)].astype(F32)
            ratio = 1.0 / read(0)
            codes = [jnp.round((read(1 + a) * ratio - read(5 + a)) * VELOCITY_CODE).astype(jnp.int32) for a in range(3)]
            codes.append(jnp.round(read(4) * ratio * ENERGY_CODE).astype(jnp.int32))
            for w in range(2):
                word = (codes[2 * w] << 16) | (codes[2 * w + 1] & 0xFFFF)
                for part in range(2):
                    at = pl.multiple_of((g * 2 + part) * 64 + c * 8, 8)
                    words[w, pl.ds(at, 8), :] = word[part * 8 : part * 8 + 8]
        for j in range(SLOTS):
            d = target[0, g * SLOTS + j]
            for w in range(2):
                ordered[d, w] = words[w, pl.ds((g * 2 + j // 8) * 64 + j % 8, 8, stride=8), :]
        return carry

    lax.fori_loop(0, groups, group, 0)
    copy = pltpu.make_async_copy(ordered, out, out_sem)
    copy.start()
    copy.wait()


def send_order(pieces, target):
    count = pieces.shape[1]
    return call(
        send_body,
        [((count, 2, 8, LANES), jnp.int32)],
        [pieces, target],
        scratch=[
            pltpu.VMEM(pieces.shape, BF16),
            pltpu.VMEM((2, count * 8, LANES), jnp.int32),
            pltpu.VMEM((count, 2, 8, LANES), jnp.int32),
            pltpu.SemaphoreType.DMA((count // SLOTS,)),
            pltpu.SemaphoreType.DMA,
        ],
        smem=(1,),
        hbm=(0,),
        hbm_outs=(0,),
        name="send_order",
        cost=3 * MIB,
    )[0]


def right_body(v, state, grad, coupling, fa, fb, fc, fd, out, states, grads, rights, span_halo, chord_halo, in_sem, out_sem):
    copies = lambda s: (
        pltpu.make_async_copy(state.at[:, s], states.at[:, s], in_sem.at[0, s]),
        pltpu.make_async_copy(grad.at[:, s], grads.at[:, s], in_sem.at[1, s]),
    )
    put_out = lambda s: pltpu.make_async_copy(rights.at[:, s], out.at[:, s], out_sem.at[s])
    for s in range(CS):
        for copy in copies(s):
            copy.start()
    unpack_faces((fa, fb, fc, fd), span_halo, chord_halo)
    field = Field(v, span_halo, chord_halo)

    def row(s, edge):
        for copy in copies(s):
            copy.wait()
        for pair in range(TILES // 2):
            wide = lambda ref, f, h: ref[f, s, wide_rows(pair), lanes(h)].astype(F32)
            fields = [[wide(states, f, h) for h in range(HALVES)] for f in range(NSTATE)]
            gradient = [[wide(grads, m, h) for h in range(HALVES)] for m in range(NCONS)]
            for part in range(2):
                t = pair * 2 + part
                cut = lambda x: x[part * 8 : part * 8 + 8]
                factors, energies, middles = [], [], []
                for h in range(HALVES):
                    ratio = 1.0 / cut(fields[0][h])
                    velocity = [cut(fields[1 + a][h]) * ratio - cut(fields[5 + a][h]) for a in range(3)]
                    factors.append([(0.5 * up, 0.5 * low) for up, low in halves_of(velocity, h)])
                    energies.append(-0.5 * (cut(fields[4][h]) * ratio))
                    size = jnp.abs(velocity[0]) + jnp.abs(velocity[1]) + jnp.abs(velocity[2])
                    middles.append(0.25 - 0.5 * size)
                base = lambda m, h, center: cut(gradient[m][h]) + middles[h] * center
                put(rights, stencil(field, s, t, edge, factors, energies, base, coupling), s, t)
        if edge >= 0:
            put_out(s - 1).start()

    each_row(row)
    put_out(CS - 1).start()
    for s in range(CS):
        put_out(s).wait()


def first_body(v, words, owner, right, coupling, fa, fb, fc, fd, out, factor, scaled, ga, gb, gc, gd, placed, rights, span_halo, chord_halo, chord_edge, word_sem, right_sem):
    per_row = owner.shape[1] // CS
    take = lambda s: pltpu.make_async_copy(right.at[:, s], rights.at[:, s], right_sem.at[s])
    landed = lambda s: placed.at[:, pl.ds(pl.multiple_of(s * per_row * 8, 8), per_row * 8)]
    whole = lambda s: pltpu.make_async_copy(landed(s), landed(s), word_sem.at[s])

    def gather(s, carry):
        for j in range(per_row):
            k = s * per_row + j
            pltpu.make_async_copy(
                words.at[owner[0, k]], placed.at[:, pl.ds(pl.multiple_of(k * 8, 8), 8)], word_sem.at[s]
            ).start()
        take(s).start()
        return carry

    lax.fori_loop(0, CS, gather, 0)
    unpack_faces((fa, fb, fc, fd), span_halo, chord_halo)
    clear_padding(chord_edge)
    field = Field(v, span_halo, chord_halo)

    def row(s, edge):
        whole(s).wait()
        take(s).wait()
        for t in range(TILES):
            factors, energies, scales = [], [], []
            for h in range(HALVES):
                pair = [placed[w, pl.ds((s * 8 + t * 2) * 8 + h, 8, stride=2), :] for w in range(2)]
                codes = []
                for word in pair:
                    codes += [(word >> 16).astype(F32), ((word << 16) >> 16).astype(F32)]
                velocity = [codes[a] * (1.0 / VELOCITY_CODE) for a in range(3)]
                size = jnp.abs(velocity[0]) + jnp.abs(velocity[1]) + jnp.abs(velocity[2])
                scale = 1.0 / (1.75 + 0.5 * size)
                half = 0.5 * scale
                pairs = [(half * up, half * low) for up, low in halves_of(velocity, h)]
                energy = (-1.0 / ENERGY_CODE) * codes[3] * half
                factors.append(pairs)
                energies.append(energy)
                scales.append(scale)
                for a in range(3):
                    factor[2 * a, s, rows(t), lanes(h)] = pairs[a][0]
                    factor[2 * a + 1, s, rows(t), lanes(h)] = pairs[a][1]
                factor[6, s, rows(t), lanes(h)] = energy

            def base(m, h, center):
                value = rights[m, s, rows(t), lanes(h)] * scales[h]
                scaled[m, s, rows(t), lanes(h)] = value
                return value

            put(out, stencil(field, s, t, edge, factors, energies, base, coupling), s, t, chord_edge)

    each_row(row)
    pack_faces(out, chord_edge, (ga, gb, gc, gd))


def sweep_row(field, factor, scaled, coupling, out, chord_edge, s, edge):
    for t in range(TILES):
        read = lambda i, h: factor[i, s, rows(t), lanes(h)]
        factors = [[(read(2 * a, h), read(2 * a + 1, h)) for a in range(3)] for h in range(HALVES)]
        energies = [read(6, h) for h in range(HALVES)]
        base = lambda m, h, center: scaled[m, s, rows(t), lanes(h)]
        put(out, stencil(field, s, t, edge, factors, energies, base, coupling), s, t, chord_edge)


def sweep_body(v, factor, scaled, coupling, fa, fb, fc, fd, out, ga, gb, gc, gd, span_halo, chord_halo, chord_edge):
    unpack_faces((fa, fb, fc, fd), span_halo, chord_halo)
    clear_padding(chord_edge)
    field = Field(v, span_halo, chord_halo)
    each_row(lambda s, edge: sweep_row(field, factor, scaled, coupling, out, chord_edge, s, edge))
    pack_faces(out, chord_edge, (ga, gb, gc, gd))


def last_body(v, factor, scaled, coupling, fa, fb, fc, fd, out, cells, span_halo, chord_halo, out_sem):
    unpack_faces((fa, fb, fc, fd), span_halo, chord_halo)
    field = Field(v, span_halo, chord_halo)
    put_out = lambda s: pltpu.make_async_copy(cells.at[:, s], out.at[:, s], out_sem.at[s])

    def row(s, edge):
        sweep_row(field, factor, scaled, coupling, cells, None, s, edge)
        if edge >= 0:
            put_out(s - 1).start()

    each_row(row)
    put_out(CS - 1).start()
    for s in range(CS):
        put_out(s).wait()


BLOCK = (NCONS, CS, CC, CN)
CELLS = (BLOCK, F32)
ROW_SEMS = pltpu.SemaphoreType.DMA((CS,))


def shards(adjoint_next, objective_grad, state_next, checkpoint_pieces, slot_target, piece_owner, coupling):
    outgoing = send_order(checkpoint_pieces, slot_target)
    incoming = lax.all_to_all(outgoing, ("span", "chord"), split_axis=0, concat_axis=0, tiled=True)
    halo = exchange(call(faces_body, FACES, [adjoint_next], scratch=[CHORD_HALO], name="faces", cost=MIB // 2))
    right = call(
        right_body,
        [CELLS],
        [adjoint_next, state_next, objective_grad, coupling, *halo],
        scratch=[
            pltpu.VMEM((NSTATE, CS, CC, CN), BF16),
            pltpu.VMEM(BLOCK, BF16),
            pltpu.VMEM(BLOCK, F32),
            SPAN_HALO,
            CHORD_HALO,
            pltpu.SemaphoreType.DMA((2, CS)),
            ROW_SEMS,
        ],
        smem=(3,),
        hbm=(1, 2),
        hbm_outs=(0,),
        name="right_side",
        cost=9 * MIB,
    )[0]
    adjoint, factor, scaled, *faces = call(
        first_body,
        [CELLS, ((7, CS, CC, CN), F32), CELLS, *FACES],
        [adjoint_next, incoming, piece_owner, right, coupling, *halo],
        scratch=[
            pltpu.VMEM((2, piece_owner.shape[1] * 8, LANES), jnp.int32),
            pltpu.VMEM(BLOCK, F32),
            SPAN_HALO,
            CHORD_HALO,
            CHORD_HALO,
            ROW_SEMS,
            ROW_SEMS,
        ],
        smem=(2, 4),
        hbm=(1, 3),
        name="first_sweep",
        cost=9 * MIB,
    )
    for sweep in range(2, SWEEPS):
        adjoint, *faces = call(
            sweep_body,
            [CELLS, *FACES],
            [adjoint, factor, scaled, coupling, *exchange(faces)],
            scratch=[SPAN_HALO, CHORD_HALO, CHORD_HALO],
            smem=(3,),
            name="sweep",
            cost=9 * MIB,
        )
    return call(
        last_body,
        [CELLS],
        [adjoint, factor, scaled, coupling, *exchange(faces)],
        scratch=[pltpu.VMEM(BLOCK, F32), SPAN_HALO, CHORD_HALO, ROW_SEMS],
        smem=(3,),
        hbm_outs=(0,),
        name="last_sweep",
        cost=9 * MIB,
    )[0]


def solution(mesh):
    placed = (
        P(None, "span", "chord", None),
        P(None, "span", "chord", None),
        P(None, "span", "chord", None),
        P(None, ("span", "chord"), None),
        P(("span", "chord"), None),
        P(("span", "chord"), None),
        P(),
    )
    return jax.shard_map(
        shards,
        mesh=mesh,
        in_specs=placed,
        out_specs=P(None, "span", "chord", None),
        check_vma=False,
    )
```

time: 122 us -> 98 us (0.80)
  starting transfers between devices: 60.4 us -> 46.2 us
  local copies, waits for them, and re-layouts: 11.3 us -> 0.82 us
  Pallas kernels: 22 us -> 28.3 us
  waiting for transfers between devices: 27.1 us -> 21.7 us
    ppermute x16, starting transfers between devices: 49.4 us -> 35.3 us  [swap(): return lax.ppermute(face, axis, pairs + [(b, a) for a, b in pairs])]
    unnamed x23 -> x8, local copies, waits for them, and re-layouts: 11.1 us -> 0.82 us
    pallas_call x6 -> x7, Pallas kernels: 22 us -> 28.3 us  [call(): pl.pallas_call(body, out_shape=[out_space(i)(shape, dtype) for i, (shape,...]
    ppermute x16, waiting for transfers between devices: 27.1 us -> 21.7 us  [swap(): return lax.ppermute(face, axis, pairs + [(b, a) for a, b in pairs])]
  transfers between devices with their start and end apart: 17 -> 17, of which waited for: 5 -> 6; matrix products, arithmetic and copies ran while one was open for 0% -> 0% of each run, Pallas kernels for 4% -> 7%
where the time goes in v1:
time: 98 us; the launch traced here: 97.2 us
  starting transfers between devices  46.2 us (47%)
  Pallas kernels  28.3 us (29%)
  waiting for transfers between devices  21.7 us (22%)
    ppermute x16, starting transfers between devices, swap(): return lax.ppermute(face, axis, pairs + [(b, a) for a, b in pairs])  35.3 us
    pallas_call x7, Pallas kernels, call(): pl.pallas_call(body, out_shape=[out_space(i)(shape, dtype) for i, (shape,...  28.3 us
    ppermute x16, waiting for transfers between devices, swap(): return lax.ppermute(face, axis, pairs + [(b, a) for a, b in pairs])  21.7 us
    all_to_all x1, starting transfers between devices, shards(): lax.all_to_all(outgoing, ('span', 'chord'), split_axis=0, concat_axis=0,...  10.9 us
  transfers between devices with their start and end apart: 17, of which 6 were waited for; matrix products, arithmetic and copies ran while one was open for 0% of the time, Pallas kernels for 7%

profile of v1, /device:TPU:39, one launch (start us, length us, event | category | flops | bytes accessed | tf_op | source)
XLA Modules:
  0.0 97.2 jit_solution(9343510933616122236)
XLA Ops:
  0.8 3.2 %send_order.1 = s32[128,2,8,128]{3,2,1,0:T(8,128)} custom-call(bf16[8,128,1024]{2,1,0:T(8,128)(2,1)} %pieces.1, s32[1,128]{1,0:T(1,128)S(1)} %copy-done.3), custom_call_target="tpu_custom_call" | custom-call | flops 25165824 | bytes 3145728 | tf_op jit(solution)/shard_map/send_order/pallas_call | solution.py:32
  4.0 10.9 %all-to-all-start = ((s32[128,2,8,128]{3,2,1,0:T(8,128)}), s32[128,2,8,128]{3,2,1,0:T(8,128)}, u32[]{:S(2)}, u32[]{:S(2)}) async-start(s32[128,2,8,128]{3,2,1,0:T(8,128)} %send_order.1), calls=%async_computation | async-start | bytes 2097152 | tf_op jit(solution)/shard_map/all_to_all | solution.py:410
  15.1 2.9 %collective-permute-start = (bf16[5,32,256]{2,1,0:T(8,128)(2,1)S(1)}, bf16[5,32,256]{2,1,0:T(8,128)(2,1)S(1)}, u32[]{:S(2)}, u32[]{:S(2)}) collective-permute-start(bf16[5,32,256]{2,1,0:T(8,128)(2,1)S(1)} %get-tuple-element.26), channel_id=1, source_target_pairs={{0,16},{32,48},{64,80},{96,112},{16,0},{48,32},{80,64},{112,96},{1... | collective-permute-start | bytes 245768 | tf_op jit(solution)/shard_map/ppermute | solution.py:119
  18.0 1.9 %collective-permute-start.1 = (bf16[5,32,256]{2,1,0:T(8,128)(2,1)S(1)}, bf16[5,32,256]{2,1,0:T(8,128)(2,1)S(1)}, u32[]{:S(2)}, u32[]{:S(2)}) collective-permute-start(bf16[5,32,256]{2,1,0:T(8,128)(2,1)S(1)} %get-tuple-element.27), channel_id=1, source_target_pairs={{16,32},{48,64},{80,96},{32,16},{64,48},{96,80},{17,33},{49,65},{8... | collective-permute-start | bytes 245768 | tf_op jit(solution)/shard_map/ppermute | solution.py:119
  20.9 3.0 %collective-permute-start.3 = (bf16[8,16,256]{2,1,0:T(8,128)(2,1)S(1)}, bf16[8,16,256]{2,1,0:T(8,128)(2,1)S(1)}, u32[]{:S(2)}, u32[]{:S(2)}) collective-permute-start(bf16[8,16,256]{2,1,0:T(8,128)(2,1)S(1)} %get-tuple-element.29), channel_id=1, source_target_pairs={{1,2},{3,4},{5,6},{7,8},{9,10},{11,12},{13,14},{2,1},{4,3},{6,5},{... | collective-permute-start | bytes 196616 | tf_op jit(solution)/shard_map/ppermute | solution.py:119
  24.0 5.3 %collective-permute-done.3.fd = bf16[8,16,256]{2,1,0:T(8,128)(2,1)S(1)} collective-permute-done((bf16[8,16,256]{2,1,0:T(8,128)(2,1)S(1)}, bf16[8,16,256]{2,1,0:T(8,128)(2,1)S(1)}, u32[]{:S(2)}, u32[]{:S(2)}) %collective-permute-start.3) | collective-permute-done | bytes 65568 | tf_op jit(solution)/shard_map/ppermute | solution.py:119
  29.2 1.7 %collective-permute-done.fa = bf16[5,32,256]{2,1,0:T(8,128)(2,1)S(1)} collective-permute-done((bf16[5,32,256]{2,1,0:T(8,128)(2,1)S(1)}, bf16[5,32,256]{2,1,0:T(8,128)(2,1)S(1)}, u32[]{:S(2)}, u32[]{:S(2)}) %collective-permute-start) | collective-permute-done | bytes 81952 | tf_op jit(solution)/shard_map/ppermute | solution.py:119
  32.3 6.8 %right_side.1.right = f32[5,16,32,256]{3,2,1,0:T(8,128)} custom-call(f32[5,16,32,256]{3,2,1,0:T(8,128)S(1)} %copy-done, bf16[8,16,32,256]{3,2,1,0:T(8,128)(2,1)} %state.1, bf16[5,16,32,256]{3,2,1,0:T(8,128)(2,1)} %grad.1, f32[5,5]{1,0:T(8,128)S(1)} %copy-done.1, bf16[5,32,256]{2,1,0:T(8,128)(2,1)S(1)} %collective-permute-done.fa, ...), custom_call_target="tpu_custom_call" | custom-call | flops 75497472 | bytes 9437184 | tf_op jit(solution)/shard_map/right_side/pallas_call | solution.py:32
  39.1 5.8 %first_sweep.1 = (f32[5,16,32,256]{3,2,1,0:T(8,128)S(1)}, f32[7,16,32,256]{3,2,1,0:T(8,128)S(1)}, f32[5,16,32,256]{3,2,1,0:T(8,128)S(1)}, bf16[5,32,256]{2,1,0:T...) custom-call(f32[5,16,32,256]{3,2,1,0:T(8,128)S(1)} %copy-done, ...), custom_call_target="tpu_custom_call" | custom-call | flops 75497472 | bytes 9437184 | tf_op jit(solution)/shard_map/first_sweep/pallas_call | solution.py:32
  44.9 1.7 %collective-permute-start.4 = (bf16[5,32,256]{2,1,0:T(8,128)(2,1)S(1)}, bf16[5,32,256]{2,1,0:T(8,128)(2,1)S(1)}, u32[]{:S(2)}, u32[]{:S(2)}) collective-permute-start(bf16[5,32,256]{2,1,0:T(8,128)(2,1)S(1)} %get-tuple-element.33), channel_id=1, source_target_pairs={{0,16},{32,48},{64,80},{96,112},{16,0},{48,32},{80,64},{112,96},{1... | collective-permute-start | bytes 245768 | tf_op jit(solution)/shard_map/ppermute | solution.py:119
  46.6 1.9 %collective-permute-start.5 = (bf16[5,32,256]{2,1,0:T(8,128)(2,1)S(1)}, bf16[5,32,256]{2,1,0:T(8,128)(2,1)S(1)}, u32[]{:S(2)}, u32[]{:S(2)}) collective-permute-start(bf16[5,32,256]{2,1,0:T(8,128)(2,1)S(1)} %get-tuple-element.34), channel_id=1, source_target_pairs={{16,32},{48,64},{80,96},{32,16},{64,48},{96,80},{17,33},{49,65},{8... | collective-permute-start | bytes 245768 | tf_op jit(solution)/shard_map/ppermute | solution.py:119
  49.6 2.8 %collective-permute-start.7 = (bf16[8,16,256]{2,1,0:T(8,128)(2,1)S(1)}, bf16[8,16,256]{2,1,0:T(8,128)(2,1)S(1)}, u32[]{:S(2)}, u32[]{:S(2)}) collective-permute-start(bf16[8,16,256]{2,1,0:T(8,128)(2,1)S(1)} %get-tuple-element.36), channel_id=1, source_target_pairs={{1,2},{3,4},{5,6},{7,8},{9,10},{11,12},{13,14},{2,1},{4,3},{6,5},{... | collective-permute-start | bytes 196616 | tf_op jit(solution)/shard_map/ppermute | solution.py:119
  52.5 4.8 %collective-permute-done.7.fd = bf16[8,16,256]{2,1,0:T(8,128)(2,1)S(1)} collective-permute-done((bf16[8,16,256]{2,1,0:T(8,128)(2,1)S(1)}, bf16[8,16,256]{2,1,0:T(8,128)(2,1)S(1)}, u32[]{:S(2)}, u32[]{:S(2)}) %collective-permute-start.7) | collective-permute-done | bytes 65568 | tf_op jit(solution)/shard_map/ppermute | solution.py:119
  57.3 3.8 %sweep.2 = (f32[5,16,32,256]{3,2,1,0:T(8,128)S(1)}, bf16[5,32,256]{2,1,0:T(8,128)(2,1)S(1)}, bf16[5,32,256]{2,1,0:T(8,128)(2,1)S(1)}, bf16[8,16,256]{2,1,0:T(8,128)(2,1)S(1)}, bf16[8,16,256]{2,1,0:T(8,128)(2,1)S(1)}) custom-call(f32[5,16,32,256]{3,2,1,0:T(8,128)S(1)} %get-tuple-element.30.v, f32[7,16,32,256]{3,2,1,0:T(8,128)S(1)} %get-tuple-element.31.factor, ...), custom_call_target="tpu_custom_call" | custom-call | flops 75497472 | bytes 9437184 | tf_op jit(solution)/shard_map/sweep/pallas_call | solution.py:32
  61.1 4.1 %collective-permute-start.8 = (bf16[5,32,256]{2,1,0:T(8,128)(2,1)S(1)}, bf16[5,32,256]{2,1,0:T(8,128)(2,1)S(1)}, u32[]{:S(2)}, u32[]{:S(2)}) collective-permute-start(bf16[5,32,256]{2,1,0:T(8,128)(2,1)S(1)} %get-tuple-element.38), channel_id=1, source_target_pairs={{0,16},{32,48},{64,80},{96,112},{16,0},{48,32},{80,64},{112,96},{1... | collective-permute-start | bytes 245768 | tf_op jit(solution)/shard_map/ppermute | solution.py:119
  65.2 1.9 %collective-permute-start.9 = (bf16[5,32,256]{2,1,0:T(8,128)(2,1)S(1)}, bf16[5,32,256]{2,1,0:T(8,128)(2,1)S(1)}, u32[]{:S(2)}, u32[]{:S(2)}) collective-permute-start(bf16[5,32,256]{2,1,0:T(8,128)(2,1)S(1)} %get-tuple-element.39), channel_id=1, source_target_pairs={{16,32},{48,64},{80,96},{32,16},{64,48},{96,80},{17,33},{49,65},{8... | collective-permute-start | bytes 245768 | tf_op jit(solution)/shard_map/ppermute | solution.py:119
  67.2 3.2 %collective-permute-start.11 = (bf16[8,16,256]{2,1,0:T(8,128)(2,1)S(1)}, bf16[8,16,256]{2,1,0:T(8,128)(2,1)S(1)}, u32[]{:S(2)}, u32[]{:S(2)}) collective-permute-start(bf16[8,16,256]{2,1,0:T(8,128)(2,1)S(1)} %get-tuple-element.41), channel_id=1, source_target_pairs={{1,2},{3,4},{5,6},{7,8},{9,10},{11,12},{13,14},{2,1},{4,3},{6,5},{... | collective-permute-start | bytes 196616 | tf_op jit(solution)/shard_map/ppermute | solution.py:119
  70.5 4.4 %collective-permute-done.11.fd = bf16[8,16,256]{2,1,0:T(8,128)(2,1)S(1)} collective-permute-done((bf16[8,16,256]{2,1,0:T(8,128)(2,1)S(1)}, bf16[8,16,256]{2,1,0:T(8,128)(2,1)S(1)}, u32[]{:S(2)}, u32[]{:S(2)}) %collective-permute-start.11) | collective-permute-done | bytes 65568 | tf_op jit(solution)/shard_map/ppermute | solution.py:119
  74.9 3.9 %sweep.3 = (f32[5,16,32,256]{3,2,1,0:T(8,128)S(1)}, bf16[5,32,256]{2,1,0:T(8,128)(2,1)S(1)}, bf16[5,32,256]{2,1,0:T(8,128)(2,1)S(1)}, bf16[8,16,256]{2,1,0:T(8,128)(2,1)S(1)}, bf16[8,16,256]{2,1,0:T(8,128)(2,1)S(1)}) custom-call(f32[5,16,32,256]{3,2,1,0:T(8,128)S(1)} %get-tuple-element.37.v, f32[7,16,32,256]{3,2,1,0:T(8,128)S(1)} %get-tuple-element.31.factor, ...), custom_call_target="tpu_custom_call" | custom-call | flops 75497472 | bytes 9437184 | tf_op jit(solution)/shard_map/sweep/pallas_call | solution.py:32
  78.9 2.7 %collective-permute-start.12 = (bf16[5,32,256]{2,1,0:T(8,128)(2,1)S(1)}, bf16[5,32,256]{2,1,0:T(8,128)(2,1)S(1)}, u32[]{:S(2)}, u32[]{:S(2)}) collective-permute-start(bf16[5,32,256]{2,1,0:T(8,128)(2,1)S(1)} %get-tuple-element.43), channel_id=1, source_target_pairs={{0,16},{32,48},{64,80},{96,112},{16,0},{48,32},{80,64},{112,96},{1... | collective-permute-start | bytes 245768 | tf_op jit(solution)/shard_map/ppermute | solution.py:119
  81.5 3.2 %collective-permute-start.13 = (bf16[5,32,256]{2,1,0:T(8,128)(2,1)S(1)}, bf16[5,32,256]{2,1,0:T(8,128)(2,1)S(1)}, u32[]{:S(2)}, u32[]{:S(2)}) collective-permute-start(bf16[5,32,256]{2,1,0:T(8,128)(2,1)S(1)} %get-tuple-element.44), channel_id=1, source_target_pairs={{16,32},{48,64},{80,96},{32,16},{64,48},{96,80},{17,33},{49,65},{8... | collective-permute-start | bytes 245768 | tf_op jit(solution)/shard_map/ppermute | solution.py:119
  84.9 3.6 %collective-permute-start.15 = (bf16[8,16,256]{2,1,0:T(8,128)(2,1)S(1)}, bf16[8,16,256]{2,1,0:T(8,128)(2,1)S(1)}, u32[]{:S(2)}, u32[]{:S(2)}) collective-permute-start(bf16[8,16,256]{2,1,0:T(8,128)(2,1)S(1)} %get-tuple-element.46), channel_id=1, source_target_pairs={{1,2},{3,4},{5,6},{7,8},{9,10},{11,12},{13,14},{2,1},{4,3},{6,5},{... | collective-permute-start | bytes 196616 | tf_op jit(solution)/shard_map/ppermute | solution.py:119
  88.5 4.1 %collective-permute-done.15.fd = bf16[8,16,256]{2,1,0:T(8,128)(2,1)S(1)} collective-permute-done((bf16[8,16,256]{2,1,0:T(8,128)(2,1)S(1)}, bf16[8,16,256]{2,1,0:T(8,128)(2,1)S(1)}, u32[]{:S(2)}, u32[]{:S(2)}) %collective-permute-start.15) | collective-permute-done | bytes 65568 | tf_op jit(solution)/shard_map/ppermute | solution.py:119
  92.6 4.7 %last_sweep.1 = f32[5,16,32,256]{3,2,1,0:T(8,128)} custom-call(f32[5,16,32,256]{3,2,1,0:T(8,128)S(1)} %get-tuple-element.42.v, f32[7,16,32,256]{3,2,1,0:T(8,128)S(1)} %get-tuple-element.31.factor, f32[5,16,32,256]{3,2,1,0:T(8,128)S(1)} %get-tuple-element.32.scaled, f32[5,5]{1,0:T(8,128)S(1)} %copy-done.1, ...), custom_call_target="tpu_custom_call" | custom-call | flops 75497472 | bytes 9437184 | tf_op jit(solution)/shard_map/last_sweep/pallas_call | solution.py:32
  (25 shorter events, 4.6 us)
Async XLA Ops:
  0.0 15.0 %copy-start = (f32[5,16,32,256]{3,2,1,0:T(8,128)S(1)}, f32[5,16,32,256]{3,2,1,0:T(8,128)}, u32[]{:S(2)}) copy-start(f32[5,16,32,256]{3,2,1,0:T(8,128)} %v.3) | copy-start | bytes 7864324
  0.0 0.8 copy-start.3
  4.0 28.3 %copy-start.1 = (f32[5,5]{1,0:T(8,128)S(1)}, f32[5,5]{1,0:T(8,128)}, u32[]{:S(2)}) copy-start(f32[5,5]{1,0:T(8,128)} %coupling.9) | copy-start | bytes 304
  4.0 35.1 %all-to-all-start = ((s32[128,2,8,128]{3,2,1,0:T(8,128)}), s32[128,2,8,128]{3,2,1,0:T(8,128)}, u32[]{:S(2)}, u32[]{:S(2)}) async-start(s32[128,2,8,128]{3,2,1,0:T(8,128)} %send_order.1), calls=%async_computation | async-start | bytes 2097152 | tf_op jit(solution)/shard_map/all_to_all | solution.py:410
  15.1 15.8 %collective-permute-start = (bf16[5,32,256]{2,1,0:T(8,128)(2,1)S(1)}, bf16[5,32,256]{2,1,0:T(8,128)(2,1)S(1)}, u32[]{:S(2)}, u32[]{:S(2)}) collective-permute-start(bf16[5,32,256]{2,1,0:T(8,128)(2,1)S(1)} %get-tuple-element.26), channel_id=1, source_target_pairs={{0,16},{32,48},{64,80},{96,112},{16,0},{48,32},{80,64},{112,96},{1... | collective-permute-start | bytes 245768 | tf_op jit(solution)/shard_map/ppermute | solution.py:119
  18.0 14.3 %collective-permute-start.1 = (bf16[5,32,256]{2,1,0:T(8,128)(2,1)S(1)}, bf16[5,32,256]{2,1,0:T(8,128)(2,1)S(1)}, u32[]{:S(2)}, u32[]{:S(2)}) collective-permute-start(bf16[5,32,256]{2,1,0:T(8,128)(2,1)S(1)} %get-tuple-element.27), channel_id=1, source_target_pairs={{16,32},{48,64},{80,96},{32,16},{64,48},{96,80},{17,33},{49,65},{8... | collective-permute-start | bytes 245768 | tf_op jit(solution)/shard_map/ppermute | solution.py:119
  19.9 4.0 %collective-permute-start.2 = (bf16[8,16,256]{2,1,0:T(8,128)(2,1)S(1)}, bf16[8,16,256]{2,1,0:T(8,128)(2,1)S(1)}, u32[]{:S(2)}, u32[]{:S(2)}) collective-permute-start(bf16[8,16,256]{2,1,0:T(8,128)(2,1)S(1)} %get-tuple-element.28), channel_id=1, source_target_pairs={{0,1},{2,3},{4,5},{6,7},{8,9},{10,11},{12,13},{14,15},{1,0},{3,2},... | collective-permute-start | bytes 196616 | tf_op jit(solution)/shard_map/ppermute | solution.py:119
  20.9 18.2 %copy-start.2 = (s32[1,128]{1,0:T(1,128)S(1)}, s32[1,128]{1,0:T(1,128)}, u32[]{:S(2)}) copy-start(s32[1,128]{1,0:T(1,128)} %owner.1) | copy-start | bytes 1540
  20.9 8.3 %collective-permute-start.3 = (bf16[8,16,256]{2,1,0:T(8,128)(2,1)S(1)}, bf16[8,16,256]{2,1,0:T(8,128)(2,1)S(1)}, u32[]{:S(2)}, u32[]{:S(2)}) collective-permute-start(bf16[8,16,256]{2,1,0:T(8,128)(2,1)S(1)} %get-tuple-element.29), channel_id=1, source_target_pairs={{1,2},{3,4},{5,6},{7,8},{9,10},{11,12},{13,14},{2,1},{4,3},{6,5},{... | collective-permute-start | bytes 196616 | tf_op jit(solution)/shard_map/ppermute | solution.py:119
  44.9 12.4 %collective-permute-start.4 = (bf16[5,32,256]{2,1,0:T(8,128)(2,1)S(1)}, bf16[5,32,256]{2,1,0:T(8,128)(2,1)S(1)}, u32[]{:S(2)}, u32[]{:S(2)}) collective-permute-start(bf16[5,32,256]{2,1,0:T(8,128)(2,1)S(1)} %get-tuple-element.33), channel_id=1, source_target_pairs={{0,16},{32,48},{64,80},{96,112},{16,0},{48,32},{80,64},{112,96},{1... | collective-permute-start | bytes 245768 | tf_op jit(solution)/shard_map/ppermute | solution.py:119
  46.6 10.7 %collective-permute-start.5 = (bf16[5,32,256]{2,1,0:T(8,128)(2,1)S(1)}, bf16[5,32,256]{2,1,0:T(8,128)(2,1)S(1)}, u32[]{:S(2)}, u32[]{:S(2)}) collective-permute-start(bf16[5,32,256]{2,1,0:T(8,128)(2,1)S(1)} %get-tuple-element.34), channel_id=1, source_target_pairs={{16,32},{48,64},{80,96},{32,16},{64,48},{96,80},{17,33},{49,65},{8... | collective-permute-start | bytes 245768 | tf_op jit(solution)/shard_map/ppermute | solution.py:119
  48.5 4.0 %collective-permute-start.6 = (bf16[8,16,256]{2,1,0:T(8,128)(2,1)S(1)}, bf16[8,16,256]{2,1,0:T(8,128)(2,1)S(1)}, u32[]{:S(2)}, u32[]{:S(2)}) collective-permute-start(bf16[8,16,256]{2,1,0:T(8,128)(2,1)S(1)} %get-tuple-element.35), channel_id=1, source_target_pairs={{0,1},{2,3},{4,5},{6,7},{8,9},{10,11},{12,13},{14,15},{1,0},{3,2},... | collective-permute-start | bytes 196616 | tf_op jit(solution)/shard_map/ppermute | solution.py:119
  49.6 7.7 %collective-permute-start.7 = (bf16[8,16,256]{2,1,0:T(8,128)(2,1)S(1)}, bf16[8,16,256]{2,1,0:T(8,128)(2,1)S(1)}, u32[]{:S(2)}, u32[]{:S(2)}) collective-permute-start(bf16[8,16,256]{2,1,0:T(8,128)(2,1)S(1)} %get-tuple-element.36), channel_id=1, source_target_pairs={{1,2},{3,4},{5,6},{7,8},{9,10},{11,12},{13,14},{2,1},{4,3},{6,5},{... | collective-permute-start | bytes 196616 | tf_op jit(solution)/shard_map/ppermute | solution.py:119
  61.1 13.8 %collective-permute-start.8 = (bf16[5,32,256]{2,1,0:T(8,128)(2,1)S(1)}, bf16[5,32,256]{2,1,0:T(8,128)(2,1)S(1)}, u32[]{:S(2)}, u32[]{:S(2)}) collective-permute-start(bf16[5,32,256]{2,1,0:T(8,128)(2,1)S(1)} %get-tuple-element.38), channel_id=1, source_target_pairs={{0,16},{32,48},{64,80},{96,112},{16,0},{48,32},{80,64},{112,96},{1... | collective-permute-start | bytes 245768 | tf_op jit(solution)/shard_map/ppermute | solution.py:119
  65.2 9.7 %collective-permute-start.9 = (bf16[5,32,256]{2,1,0:T(8,128)(2,1)S(1)}, bf16[5,32,256]{2,1,0:T(8,128)(2,1)S(1)}, u32[]{:S(2)}, u32[]{:S(2)}) collective-permute-start(bf16[5,32,256]{2,1,0:T(8,128)(2,1)S(1)} %get-tuple-element.39), channel_id=1, source_target_pairs={{16,32},{48,64},{80,96},{32,16},{64,48},{96,80},{17,33},{49,65},{8... | collective-permute-start | bytes 245768 | tf_op jit(solution)/shard_map/ppermute | solution.py:119
  67.1 3.3 %collective-permute-start.10 = (bf16[8,16,256]{2,1,0:T(8,128)(2,1)S(1)}, bf16[8,16,256]{2,1,0:T(8,128)(2,1)S(1)}, u32[]{:S(2)}, u32[]{:S(2)}) collective-permute-start(bf16[8,16,256]{2,1,0:T(8,128)(2,1)S(1)} %get-tuple-element.40), channel_id=1, source_target_pairs={{0,1},{2,3},{4,5},{6,7},{8,9},{10,11},{12,13},{14,15},{1,0},{3,2},... | collective-permute-start | bytes 196616 | tf_op jit(solution)/shard_map/ppermute | solution.py:119
  67.2 7.7 %collective-permute-start.11 = (bf16[8,16,256]{2,1,0:T(8,128)(2,1)S(1)}, bf16[8,16,256]{2,1,0:T(8,128)(2,1)S(1)}, u32[]{:S(2)}, u32[]{:S(2)}) collective-permute-start(bf16[8,16,256]{2,1,0:T(8,128)(2,1)S(1)} %get-tuple-element.41), channel_id=1, source_target_pairs={{1,2},{3,4},{5,6},{7,8},{9,10},{11,12},{13,14},{2,1},{4,3},{6,5},{... | collective-permute-start | bytes 196616 | tf_op jit(solution)/shard_map/ppermute | solution.py:119
  78.9 13.7 %collective-permute-start.12 = (bf16[5,32,256]{2,1,0:T(8,128)(2,1)S(1)}, bf16[5,32,256]{2,1,0:T(8,128)(2,1)S(1)}, u32[]{:S(2)}, u32[]{:S(2)}) collective-permute-start(bf16[5,32,256]{2,1,0:T(8,128)(2,1)S(1)} %get-tuple-element.43), channel_id=1, source_target_pairs={{0,16},{32,48},{64,80},{96,112},{16,0},{48,32},{80,64},{112,96},{1... | collective-permute-start | bytes 245768 | tf_op jit(solution)/shard_map/ppermute | solution.py:119
  81.5 11.0 %collective-permute-start.13 = (bf16[5,32,256]{2,1,0:T(8,128)(2,1)S(1)}, bf16[5,32,256]{2,1,0:T(8,128)(2,1)S(1)}, u32[]{:S(2)}, u32[]{:S(2)}) collective-permute-start(bf16[5,32,256]{2,1,0:T(8,128)(2,1)S(1)} %get-tuple-element.44), channel_id=1, source_target_pairs={{16,32},{48,64},{80,96},{32,16},{64,48},{96,80},{17,33},{49,65},{8... | collective-permute-start | bytes 245768 | tf_op jit(solution)/shard_map/ppermute | solution.py:119
  84.8 3.7 %collective-permute-start.14 = (bf16[8,16,256]{2,1,0:T(8,128)(2,1)S(1)}, bf16[8,16,256]{2,1,0:T(8,128)(2,1)S(1)}, u32[]{:S(2)}, u32[]{:S(2)}) collective-permute-start(bf16[8,16,256]{2,1,0:T(8,128)(2,1)S(1)} %get-tuple-element.45), channel_id=1, source_target_pairs={{0,1},{2,3},{4,5},{6,7},{8,9},{10,11},{12,13},{14,15},{1,0},{3,2},... | collective-permute-start | bytes 196616 | tf_op jit(solution)/shard_map/ppermute | solution.py:119
  84.9 7.7 %collective-permute-start.15 = (bf16[8,16,256]{2,1,0:T(8,128)(2,1)S(1)}, bf16[8,16,256]{2,1,0:T(8,128)(2,1)S(1)}, u32[]{:S(2)}, u32[]{:S(2)}) collective-permute-start(bf16[8,16,256]{2,1,0:T(8,128)(2,1)S(1)} %get-tuple-element.46), channel_id=1, source_target_pairs={{1,2},{3,4},{5,6},{7,8},{9,10},{11,12},{13,14},{2,1},{4,3},{6,5},{... | collective-permute-start | bytes 196616 | tf_op jit(solution)/shard_map/ppermute | solution.py:119

commit v2 on v1

--- a/solution.py
+++ b/solution.py
@@ -17,6 +17,7 @@
 HALVES = CN // LANES
 VELOCITY_CODE = 4368.0
 ENERGY_CODE = 8190.0
+ADJOINT_CODE = 5461.0
 MIB = 1 << 20
 F32 = jnp.float32
 BF16 = jnp.bfloat16
@@ -97,6 +98,49 @@
             face[group] = jnp.concatenate(both, axis=0).astype(BF16)
 
 
+def code_pair(high, low, scale):
+    code = lambda x: jnp.round(x * scale).astype(jnp.int32)
+    return (code(high) << 16) | (code(low) & 0xFFFF)
+
+
+def decode_pair(word):
+    return (word >> 16).astype(F32), ((word << 16) >> 16).astype(F32)
+
+
+START_SPAN = ((NCONS, CC // 2, CN), jnp.int32)
+START_CHORD = ((CS // 2, 8, CN), jnp.int32)
+START_FACES = [START_SPAN, START_SPAN, START_CHORD, START_CHORD]
+
+
+def pack_start(cells, chord_edge, faces):
+    span_a, span_b, chord_a, chord_b = faces
+    p = parity("span")
+    for face, side in ((span_a, 1 - p), (span_b, p)):
+        for m in range(NCONS):
+            for pair in range(CC // 16):
+                high, low = (cells[m, side * (CS - 1), rows(2 * pair + i), :] for i in range(2))
+                face[m, rows(pair), :] = code_pair(high, low, ADJOINT_CODE)
+    p = parity("chord")
+    for face, side in ((chord_a, 1 - p), (chord_b, p)):
+        for group in range(CS // 2):
+            face[group] = code_pair(chord_edge[side, 2 * group], chord_edge[side, 2 * group + 1], ADJOINT_CODE)
+
+
+def unpack_start(faces, span_halo, chord_halo):
+    span_a, span_b, chord_a, chord_b = faces
+    p = parity("span")
+    for face, side in ((span_a, 1 - p), (span_b, p)):
+        for m in range(NCONS):
+            for pair in range(CC // 16):
+                for i, half in enumerate(decode_pair(face[m, rows(pair), :])):
+                    span_halo[side, m, rows(2 * pair + i), :] = half * (1.0 / ADJOINT_CODE)
+    p = parity("chord")
+    for face, side in ((chord_a, 1 - p), (chord_b, p)):
+        for group in range(CS // 2):
+            for i, half in enumerate(decode_pair(face[group])):
+                chord_halo[side, 2 * group + i] = half * (1.0 / ADJOINT_CODE)
+
+
 def clear_padding(chord_edge):
     for side in range(2):
         for s in range(CS):
@@ -109,7 +153,7 @@
         for m in range(NCONS):
             chord_edge[0, s, pl.ds(m, 1), :] = cells[m, s, pl.ds(0, 1), :]
             chord_edge[1, s, pl.ds(m, 1), :] = cells[m, s, pl.ds(CC - 1, 1), :]
-    pack_faces(cells, chord_edge, (span_a, span_b, chord_a, chord_b))
+    pack_start(cells, chord_edge, (span_a, span_b, chord_a, chord_b))
 
 
 def exchange(faces):
@@ -119,11 +163,15 @@
         return lax.ppermute(face, axis, pairs + [(b, a) for a, b in pairs])
 
     span_a, span_b, chord_a, chord_b = faces
-    return swap(span_a, "span", 0), swap(span_b, "span", 1), swap(chord_a, "chord", 0), swap(chord_b, "chord", 1)
+    span_b = swap(span_b, "span", 1)
+    span_a = swap(span_a, "span", 0)
+    chord_b = swap(chord_b, "chord", 1)
+    chord_a = swap(chord_a, "chord", 0)
+    return span_a, span_b, chord_a, chord_b
 
 
 class Field:
-    def __init__(self, cells, span_halo, chord_halo):
+    def __init__(self, cells, span_halo=None, chord_halo=None):
         self.cells = cells
         self.span_halo = span_halo
         self.chord_halo = chord_halo
@@ -132,11 +180,15 @@
         return self.cells[m, s, rows(t), lanes(h)]
 
     def span(self, m, s, t, h, step, edge):
+        if edge == step and self.span_halo is None:
+            return jnp.zeros((8, LANES), F32)
         if edge == step:
             return self.span_halo[1 if step > 0 else 0, m, rows(t), lanes(h)]
         return self.cells[m, s + step, rows(t), lanes(h)]
 
     def beyond(self, side, m, s, h):
+        if self.chord_halo is None:
+            return jnp.zeros((8, LANES), F32)
         return jnp.broadcast_to(self.chord_halo[side, s, pl.ds(m, 1), lanes(h)], (8, LANES))
 
     def chord(self, m, s, t, h, step, center, first, last):
@@ -271,7 +323,7 @@
     )[0]
 
 
-def right_body(v, state, grad, coupling, fa, fb, fc, fd, out, states, grads, rights, span_halo, chord_halo, in_sem, out_sem):
+def right_body(v, state, grad, coupling, out, span_next, chord_next, states, grads, rights, in_sem, out_sem):
     copies = lambda s: (
         pltpu.make_async_copy(state.at[:, s], states.at[:, s], in_sem.at[0, s]),
         pltpu.make_async_copy(grad.at[:, s], grads.at[:, s], in_sem.at[1, s]),
@@ -280,8 +332,8 @@
     for s in range(CS):
         for copy in copies(s):
             copy.start()
-    unpack_faces((fa, fb, fc, fd), span_halo, chord_halo)
-    field = Field(v, span_halo, chord_halo)
+    field = Field(v)
+    row_first, row_last = mask_of(0, 0), mask_of(0, 7)
 
     def row(s, edge):
         for copy in copies(s):
@@ -301,6 +353,15 @@
                     energies.append(-0.5 * (cut(fields[4][h]) * ratio))
                     size = jnp.abs(velocity[0]) + jnp.abs(velocity[1]) + jnp.abs(velocity[2])
                     middles.append(0.25 - 0.5 * size)
+                    (span_up, span_low), (chord_up, chord_low), _ = factors[h]
+                    if edge == -1:
+                        span_next[0, rows(t), lanes(h)] = span_low
+                    if edge == 1:
+                        span_next[1, rows(t), lanes(h)] = span_up
+                    if t == 0:
+                        chord_next[0, s, :, lanes(h)] = jnp.where(row_first, chord_low, 0.0)
+                    if t == TILES - 1:
+                        chord_next[1, s, :, lanes(h)] = jnp.where(row_last, chord_up, 0.0)
                 base = lambda m, h, center: cut(gradient[m][h]) + middles[h] * center
                 put(rights, stencil(field, s, t, edge, factors, energies, base, coupling), s, t)
         if edge >= 0:
@@ -312,7 +373,7 @@
         put_out(s).wait()
 
 
-def first_body(v, words, owner, right, coupling, fa, fb, fc, fd, out, factor, scaled, ga, gb, gc, gd, placed, rights, span_halo, chord_halo, chord_edge, word_sem, right_sem):
+def first_body(v, words, owner, right, coupling, span_next, chord_next, fa, fb, fc, fd, out, factor, scaled, ga, gb, gc, gd, placed, rights, span_halo, chord_halo, chord_edge, word_sem, right_sem):
     per_row = owner.shape[1] // CS
     take = lambda s: pltpu.make_async_copy(right.at[:, s], rights.at[:, s], right_sem.at[s])
     landed = lambda s: placed.at[:, pl.ds(pl.multiple_of(s * per_row * 8, 8), per_row * 8)]
@@ -328,7 +389,7 @@
         return carry
 
     lax.fori_loop(0, CS, gather, 0)
-    unpack_faces((fa, fb, fc, fd), span_halo, chord_halo)
+    unpack_start((fa, fb, fc, fd), span_halo, chord_halo)
     clear_padding(chord_edge)
     field = Field(v, span_halo, chord_halo)
 
@@ -339,9 +400,7 @@
             factors, energies, scales = [], [], []
             for h in range(HALVES):
                 pair = [placed[w, pl.ds((s * 8 + t * 2) * 8 + h, 8, stride=2), :] for w in range(2)]
-                codes = []
-                for word in pair:
-                    codes += [(word >> 16).astype(F32), ((word << 16) >> 16).astype(F32)]
+                codes = [*decode_pair(pair[0]), *decode_pair(pair[1])]
                 velocity = [codes[a] * (1.0 / VELOCITY_CODE) for a in range(3)]
                 size = jnp.abs(velocity[0]) + jnp.abs(velocity[1]) + jnp.abs(velocity[2])
                 scale = 1.0 / (1.75 + 0.5 * size)
@@ -357,7 +416,15 @@
                 factor[6, s, rows(t), lanes(h)] = energy
 
             def base(m, h, center):
-                value = rights[m, s, rows(t), lanes(h)] * scales[h]
+                value = rights[m, s, rows(t), lanes(h)]
+                if edge != 0:
+                    side = 0 if edge == -1 else 1
+                    value = value + span_next[side, rows(t), lanes(h)] * span_halo[side, m, rows(t), lanes(h)]
+                if t == 0:
+                    value = value + chord_next[0, s, :, lanes(h)] * field.beyond(0, m, s, h)
+                if t == TILES - 1:
+                    value = value + chord_next[1, s, :, lanes(h)] * field.beyond(1, m, s, h)
+                value = value * scales[h]
                 scaled[m, s, rows(t), lanes(h)] = value
                 return value
 
@@ -408,17 +475,15 @@
 def shards(adjoint_next, objective_grad, state_next, checkpoint_pieces, slot_target, piece_owner, coupling):
     outgoing = send_order(checkpoint_pieces, slot_target)
     incoming = lax.all_to_all(outgoing, ("span", "chord"), split_axis=0, concat_axis=0, tiled=True)
-    halo = exchange(call(faces_body, FACES, [adjoint_next], scratch=[CHORD_HALO], name="faces", cost=MIB // 2))
-    right = call(
+    halo = exchange(call(faces_body, START_FACES, [adjoint_next], scratch=[CHORD_HALO], name="faces", cost=MIB // 2))
+    right, span_next, chord_next = call(
         right_body,
-        [CELLS],
-        [adjoint_next, state_next, objective_grad, coupling, *halo],
+        [CELLS, ((2, CC, CN), F32), ((2, CS, 8, CN), F32)],
+        [adjoint_next, state_next, objective_grad, coupling],
         scratch=[
             pltpu.VMEM((NSTATE, CS, CC, CN), BF16),
             pltpu.VMEM(BLOCK, BF16),
             pltpu.VMEM(BLOCK, F32),
-            SPAN_HALO,
-            CHORD_HALO,
             pltpu.SemaphoreType.DMA((2, CS)),
             ROW_SEMS,
         ],
@@ -427,11 +492,11 @@
         hbm_outs=(0,),
         name="right_side",
         cost=9 * MIB,
-    )[0]
+    )
     adjoint, factor, scaled, *faces = call(
         first_body,
         [CELLS, ((7, CS, CC, CN), F32), CELLS, *FACES],
-        [adjoint_next, incoming, piece_owner, right, coupling, *halo],
+        [adjoint_next, incoming, piece_owner, right, coupling, span_next, chord_next, *halo],
         scratch=[
             pltpu.VMEM((2, piece_owner.shape[1] * 8, LANES), jnp.int32),
             pltpu.VMEM(BLOCK, F32),

time: 98 us -> 92.5 us (0.944); the launches traced: 97.2 us -> 90.7 us
  waiting for transfers between devices: 21.7 us -> 11.5 us
  starting transfers between devices: 46.2 us -> 50 us
    ppermute x16, waiting for transfers between devices: 21.7 us -> 11.5 us  [swap(): return lax.ppermute(face, axis, pairs + [(b, a) for a, b in pairs])]
    ppermute x16, starting transfers between devices: 35.3 us -> 39 us  [swap(): return lax.ppermute(face, axis, pairs + [(b, a) for a, b in pairs])]
  transfers between devices with their start and end apart: 17 -> 17, of which waited for: 6 -> 5; matrix products, arithmetic and copies ran while one was open for 0% -> 0% of each run, Pallas kernels for 7% -> 8%
where the time goes in v2:
time: 92.5 us; the launch traced here: 90.7 us
  starting transfers between devices  50 us (54%)
  Pallas kernels  28.2 us (30%)
  waiting for transfers between devices  11.5 us (12%)
    ppermute x16, starting transfers between devices, swap(): return lax.ppermute(face, axis, pairs + [(b, a) for a, b in pairs])  39 us
    pallas_call x7, Pallas kernels, call(): pl.pallas_call(body, out_shape=[out_space(i)(shape, dtype) for i, (shape,...  28.2 us
    ppermute x16, waiting for transfers between devices, swap(): return lax.ppermute(face, axis, pairs + [(b, a) for a, b in pairs])  11.5 us
    all_to_all x1, starting transfers between devices, shards(): lax.all_to_all(outgoing, ('span', 'chord'), split_axis=0, concat_axis=0,...  10.9 us
  transfers between devices with their start and end apart: 17, of which 5 were waited for; matrix products, arithmetic and copies ran while one was open for 0% of the time, Pallas kernels for 8%

profile of v2, /device:TPU:39, one launch (start us, length us, event | category | flops | bytes accessed | tf_op | source)
XLA Modules:
  0.0 90.7 jit_solution(2246935901626875413)
XLA Ops:
  0.8 3.2 %send_order.1 = s32[128,2,8,128]{3,2,1,0:T(8,128)} custom-call(bf16[8,128,1024]{2,1,0:T(8,128)(2,1)} %pieces.1, s32[1,128]{1,0:T(1,128)S(1)} %copy-done.3), custom_call_target="tpu_custom_call" | custom-call | flops 25165824 | bytes 3145728 | tf_op jit(solution)/shard_map/send_order/pallas_call | solution.py:33
  4.0 10.9 %all-to-all-start = ((s32[128,2,8,128]{3,2,1,0:T(8,128)}), s32[128,2,8,128]{3,2,1,0:T(8,128)}, u32[]{:S(2)}, u32[]{:S(2)}) async-start(s32[128,2,8,128]{3,2,1,0:T(8,128)} %send_order.1), calls=%async_computation | async-start | bytes 2097152 | tf_op jit(solution)/shard_map/all_to_all | solution.py:477
  15.1 2.9 %collective-permute-start = (s32[5,16,256]{2,1,0:T(8,128)S(1)}, s32[5,16,256]{2,1,0:T(8,128)S(1)}, u32[]{:S(2)}, u32[]{:S(2)}) collective-permute-start(s32[5,16,256]{2,1,0:T(8,128)S(1)} %get-tuple-element.32), channel_id=1, source_target_pairs={{0,16},{32,48},{64,80},{96,112},{16,0},{48,32},{80,64},{112,96},{1... | collective-permute-start | bytes 245768 | tf_op jit(solution)/shard_map/ppermute | solution.py:163
  18.0 1.9 %collective-permute-start.1 = (s32[5,16,256]{2,1,0:T(8,128)S(1)}, s32[5,16,256]{2,1,0:T(8,128)S(1)}, u32[]{:S(2)}, u32[]{:S(2)}) collective-permute-start(s32[5,16,256]{2,1,0:T(8,128)S(1)} %get-tuple-element.33), channel_id=1, source_target_pairs={{16,32},{48,64},{80,96},{32,16},{64,48},{96,80},{17,33},{49,65},{8... | collective-permute-start | bytes 245768 | tf_op jit(solution)/shard_map/ppermute | solution.py:163
  21.0 3.0 %collective-permute-start.3 = (s32[8,8,256]{2,1,0:T(8,128)S(1)}, s32[8,8,256]{2,1,0:T(8,128)S(1)}, u32[]{:S(2)}, u32[]{:S(2)}) collective-permute-start(s32[8,8,256]{2,1,0:T(8,128)S(1)} %get-tuple-element.35), channel_id=1, source_target_pairs={{1,2},{3,4},{5,6},{7,8},{9,10},{11,12},{13,14},{2,1},{4,3},{6,5},{... | collective-permute-start | bytes 196616 | tf_op jit(solution)/shard_map/ppermute | solution.py:163
  24.0 6.8 %right_side.1 = (f32[5,16,32,256]{3,2,1,0:T(8,128)}, f32[2,32,256]{2,1,0:T(8,128)S(1)}, f32[2,16,8,256]{3,2,1,0:T(8,128)S(1)}) custom-call(f32[5,16,32,256]{3,2,1,0:T(8,128)S(1)} %copy-done, bf16[8,16,32,256]{3,2,1,0:T(8,128)(2,1)} %state.1, bf16[5,16,32,256]{3,2,1,0:T(8,128)(2,1)} %grad.1, f32[5,5]{1,0:T(8,128)S(1)} %copy-done.1), custom_call_target="tpu_custom_call" | custom-call | flops 75497472 | bytes 9437184 | tf_op jit(solution)/shard_map/right_side/pallas_call | solution.py:33
  30.9 1.4 %collective-permute-done.1.fb = s32[5,16,256]{2,1,0:T(8,128)S(1)} collective-permute-done((s32[5,16,256]{2,1,0:T(8,128)S(1)}, s32[5,16,256]{2,1,0:T(8,128)S(1)}, u32[]{:S(2)}, u32[]{:S(2)}) %collective-permute-start.1) | collective-permute-done | bytes 81952 | tf_op jit(solution)/shard_map/ppermute | solution.py:163
  32.3 5.9 %first_sweep.1 = (f32[5,16,32,256]{3,2,1,0:T(8,128)S(1)}, f32[7,16,32,256]{3,2,1,0:T(8,128)S(1)}, f32[5,16,32,256]{3,2,1,0:T(8,128)S(1)}, bf16[5,32,256]{2,1,0:T...) custom-call(f32[5,16,32,256]{3,2,1,0:T(8,128)S(1)} %copy-done, ...), custom_call_target="tpu_custom_call" | custom-call | flops 75497472 | bytes 9437184 | tf_op jit(solution)/shard_map/first_sweep/pallas_call | solution.py:33
  38.2 2.5 %collective-permute-start.4 = (bf16[5,32,256]{2,1,0:T(8,128)(2,1)S(1)}, bf16[5,32,256]{2,1,0:T(8,128)(2,1)S(1)}, u32[]{:S(2)}, u32[]{:S(2)}) collective-permute-start(bf16[5,32,256]{2,1,0:T(8,128)(2,1)S(1)} %get-tuple-element.39), channel_id=1, source_target_pairs={{0,16},{32,48},{64,80},{96,112},{16,0},{48,32},{80,64},{112,96},{1... | collective-permute-start | bytes 245768 | tf_op jit(solution)/shard_map/ppermute | solution.py:163
  40.7 1.9 %collective-permute-start.5 = (bf16[5,32,256]{2,1,0:T(8,128)(2,1)S(1)}, bf16[5,32,256]{2,1,0:T(8,128)(2,1)S(1)}, u32[]{:S(2)}, u32[]{:S(2)}) collective-permute-start(bf16[5,32,256]{2,1,0:T(8,128)(2,1)S(1)} %get-tuple-element.40), channel_id=1, source_target_pairs={{16,32},{48,64},{80,96},{32,16},{64,48},{96,80},{17,33},{49,65},{8... | collective-permute-start | bytes 245768 | tf_op jit(solution)/shard_map/ppermute | solution.py:163
  42.6 1.6 %collective-permute-start.6 = (bf16[8,16,256]{2,1,0:T(8,128)(2,1)S(1)}, bf16[8,16,256]{2,1,0:T(8,128)(2,1)S(1)}, u32[]{:S(2)}, u32[]{:S(2)}) collective-permute-start(bf16[8,16,256]{2,1,0:T(8,128)(2,1)S(1)} %get-tuple-element.41), channel_id=1, source_target_pairs={{0,1},{2,3},{4,5},{6,7},{8,9},{10,11},{12,13},{14,15},{1,0},{3,2},... | collective-permute-start | bytes 196616 | tf_op jit(solution)/shard_map/ppermute | solution.py:163
  44.1 3.5 %collective-permute-start.7 = (bf16[8,16,256]{2,1,0:T(8,128)(2,1)S(1)}, bf16[8,16,256]{2,1,0:T(8,128)(2,1)S(1)}, u32[]{:S(2)}, u32[]{:S(2)}) collective-permute-start(bf16[8,16,256]{2,1,0:T(8,128)(2,1)S(1)} %get-tuple-element.42), channel_id=1, source_target_pairs={{1,2},{3,4},{5,6},{7,8},{9,10},{11,12},{13,14},{2,1},{4,3},{6,5},{... | collective-permute-start | bytes 196616 | tf_op jit(solution)/shard_map/ppermute | solution.py:163
  47.7 4.1 %collective-permute-done.7.fd = bf16[8,16,256]{2,1,0:T(8,128)(2,1)S(1)} collective-permute-done((bf16[8,16,256]{2,1,0:T(8,128)(2,1)S(1)}, bf16[8,16,256]{2,1,0:T(8,128)(2,1)S(1)}, u32[]{:S(2)}, u32[]{:S(2)}) %collective-permute-start.7) | collective-permute-done | bytes 65568 | tf_op jit(solution)/shard_map/ppermute | solution.py:163
  51.8 3.8 %sweep.2 = (f32[5,16,32,256]{3,2,1,0:T(8,128)S(1)}, bf16[5,32,256]{2,1,0:T(8,128)(2,1)S(1)}, bf16[5,32,256]{2,1,0:T(8,128)(2,1)S(1)}, bf16[8,16,256]{2,1,0:T(8,128)(2,1)S(1)}, bf16[8,16,256]{2,1,0:T(8,128)(2,1)S(1)}) custom-call(f32[5,16,32,256]{3,2,1,0:T(8,128)S(1)} %get-tuple-element.36.v, f32[7,16,32,256]{3,2,1,0:T(8,128)S(1)} %get-tuple-element.37.factor, ...), custom_call_target="tpu_custom_call" | custom-call | flops 75497472 | bytes 9437184 | tf_op jit(solution)/shard_map/sweep/pallas_call | solution.py:33
  55.6 3.2 %collective-permute-start.8 = (bf16[5,32,256]{2,1,0:T(8,128)(2,1)S(1)}, bf16[5,32,256]{2,1,0:T(8,128)(2,1)S(1)}, u32[]{:S(2)}, u32[]{:S(2)}) collective-permute-start(bf16[5,32,256]{2,1,0:T(8,128)(2,1)S(1)} %get-tuple-element.44), channel_id=1, source_target_pairs={{0,16},{32,48},{64,80},{96,112},{16,0},{48,32},{80,64},{112,96},{1... | collective-permute-start | bytes 245768 | tf_op jit(solution)/shard_map/ppermute | solution.py:163
  58.9 1.9 %collective-permute-start.9 = (bf16[5,32,256]{2,1,0:T(8,128)(2,1)S(1)}, bf16[5,32,256]{2,1,0:T(8,128)(2,1)S(1)}, u32[]{:S(2)}, u32[]{:S(2)}) collective-permute-start(bf16[5,32,256]{2,1,0:T(8,128)(2,1)S(1)} %get-tuple-element.45), channel_id=1, source_target_pairs={{16,32},{48,64},{80,96},{32,16},{64,48},{96,80},{17,33},{49,65},{8... | collective-permute-start | bytes 245768 | tf_op jit(solution)/shard_map/ppermute | solution.py:163
  60.9 4.5 %collective-permute-start.11 = (bf16[8,16,256]{2,1,0:T(8,128)(2,1)S(1)}, bf16[8,16,256]{2,1,0:T(8,128)(2,1)S(1)}, u32[]{:S(2)}, u32[]{:S(2)}) collective-permute-start(bf16[8,16,256]{2,1,0:T(8,128)(2,1)S(1)} %get-tuple-element.47), channel_id=1, source_target_pairs={{1,2},{3,4},{5,6},{7,8},{9,10},{11,12},{13,14},{2,1},{4,3},{6,5},{... | collective-permute-start | bytes 196616 | tf_op jit(solution)/shard_map/ppermute | solution.py:163
  65.4 3.2 %collective-permute-done.11.fd = bf16[8,16,256]{2,1,0:T(8,128)(2,1)S(1)} collective-permute-done((bf16[8,16,256]{2,1,0:T(8,128)(2,1)S(1)}, bf16[8,16,256]{2,1,0:T(8,128)(2,1)S(1)}, u32[]{:S(2)}, u32[]{:S(2)}) %collective-permute-start.11) | collective-permute-done | bytes 65568 | tf_op jit(solution)/shard_map/ppermute | solution.py:163
  68.6 3.8 %sweep.3 = (f32[5,16,32,256]{3,2,1,0:T(8,128)S(1)}, bf16[5,32,256]{2,1,0:T(8,128)(2,1)S(1)}, bf16[5,32,256]{2,1,0:T(8,128)(2,1)S(1)}, bf16[8,16,256]{2,1,0:T(8,128)(2,1)S(1)}, bf16[8,16,256]{2,1,0:T(8,128)(2,1)S(1)}) custom-call(f32[5,16,32,256]{3,2,1,0:T(8,128)S(1)} %get-tuple-element.43.v, f32[7,16,32,256]{3,2,1,0:T(8,128)S(1)} %get-tuple-element.37.factor, ...), custom_call_target="tpu_custom_call" | custom-call | flops 75497472 | bytes 9437184 | tf_op jit(solution)/shard_map/sweep/pallas_call | solution.py:33
  72.4 2.3 %collective-permute-start.12 = (bf16[5,32,256]{2,1,0:T(8,128)(2,1)S(1)}, bf16[5,32,256]{2,1,0:T(8,128)(2,1)S(1)}, u32[]{:S(2)}, u32[]{:S(2)}) collective-permute-start(bf16[5,32,256]{2,1,0:T(8,128)(2,1)S(1)} %get-tuple-element.49), channel_id=1, source_target_pairs={{0,16},{32,48},{64,80},{96,112},{16,0},{48,32},{80,64},{112,96},{1... | collective-permute-start | bytes 245768 | tf_op jit(solution)/shard_map/ppermute | solution.py:163
  74.7 3.5 %collective-permute-start.13 = (bf16[5,32,256]{2,1,0:T(8,128)(2,1)S(1)}, bf16[5,32,256]{2,1,0:T(8,128)(2,1)S(1)}, u32[]{:S(2)}, u32[]{:S(2)}) collective-permute-start(bf16[5,32,256]{2,1,0:T(8,128)(2,1)S(1)} %get-tuple-element.50), channel_id=1, source_target_pairs={{16,32},{48,64},{80,96},{32,16},{64,48},{96,80},{17,33},{49,65},{8... | collective-permute-start | bytes 245768 | tf_op jit(solution)/shard_map/ppermute | solution.py:163
  78.3 5.1 %collective-permute-start.15 = (bf16[8,16,256]{2,1,0:T(8,128)(2,1)S(1)}, bf16[8,16,256]{2,1,0:T(8,128)(2,1)S(1)}, u32[]{:S(2)}, u32[]{:S(2)}) collective-permute-start(bf16[8,16,256]{2,1,0:T(8,128)(2,1)S(1)} %get-tuple-element.52), channel_id=1, source_target_pairs={{1,2},{3,4},{5,6},{7,8},{9,10},{11,12},{13,14},{2,1},{4,3},{6,5},{... | collective-permute-start | bytes 196616 | tf_op jit(solution)/shard_map/ppermute | solution.py:163
  83.5 2.6 %collective-permute-done.15.fd = bf16[8,16,256]{2,1,0:T(8,128)(2,1)S(1)} collective-permute-done((bf16[8,16,256]{2,1,0:T(8,128)(2,1)S(1)}, bf16[8,16,256]{2,1,0:T(8,128)(2,1)S(1)}, u32[]{:S(2)}, u32[]{:S(2)}) %collective-permute-start.15) | collective-permute-done | bytes 65568 | tf_op jit(solution)/shard_map/ppermute | solution.py:163
  86.0 4.7 %last_sweep.1 = f32[5,16,32,256]{3,2,1,0:T(8,128)} custom-call(f32[5,16,32,256]{3,2,1,0:T(8,128)S(1)} %get-tuple-element.48.v, f32[7,16,32,256]{3,2,1,0:T(8,128)S(1)} %get-tuple-element.37.factor, f32[5,16,32,256]{3,2,1,0:T(8,128)S(1)} %get-tuple-element.38.scaled, f32[5,5]{1,0:T(8,128)S(1)} %copy-done.1, ...), custom_call_target="tpu_custom_call" | custom-call | flops 75497472 | bytes 9437184 | tf_op jit(solution)/shard_map/last_sweep/pallas_call | solution.py:33
  (25 shorter events, 2.3 us)
Async XLA Ops:
  0.0 15.0 %copy-start = (f32[5,16,32,256]{3,2,1,0:T(8,128)S(1)}, f32[5,16,32,256]{3,2,1,0:T(8,128)}, u32[]{:S(2)}) copy-start(f32[5,16,32,256]{3,2,1,0:T(8,128)} %v.3) | copy-start | bytes 7864324
  0.0 0.8 copy-start.3
  4.0 20.0 %copy-start.1 = (f32[5,5]{1,0:T(8,128)S(1)}, f32[5,5]{1,0:T(8,128)}, u32[]{:S(2)}) copy-start(f32[5,5]{1,0:T(8,128)} %coupling.9) | copy-start | bytes 304
  4.0 28.3 %all-to-all-start = ((s32[128,2,8,128]{3,2,1,0:T(8,128)}), s32[128,2,8,128]{3,2,1,0:T(8,128)}, u32[]{:S(2)}, u32[]{:S(2)}) async-start(s32[128,2,8,128]{3,2,1,0:T(8,128)} %send_order.1), calls=%async_computation | async-start | bytes 2097152 | tf_op jit(solution)/shard_map/all_to_all | solution.py:477
  15.1 15.8 %collective-permute-start = (s32[5,16,256]{2,1,0:T(8,128)S(1)}, s32[5,16,256]{2,1,0:T(8,128)S(1)}, u32[]{:S(2)}, u32[]{:S(2)}) collective-permute-start(s32[5,16,256]{2,1,0:T(8,128)S(1)} %get-tuple-element.32), channel_id=1, source_target_pairs={{0,16},{32,48},{64,80},{96,112},{16,0},{48,32},{80,64},{112,96},{1... | collective-permute-start | bytes 245768 | tf_op jit(solution)/shard_map/ppermute | solution.py:163
  18.0 14.3 %collective-permute-start.1 = (s32[5,16,256]{2,1,0:T(8,128)S(1)}, s32[5,16,256]{2,1,0:T(8,128)S(1)}, u32[]{:S(2)}, u32[]{:S(2)}) collective-permute-start(s32[5,16,256]{2,1,0:T(8,128)S(1)} %get-tuple-element.33), channel_id=1, source_target_pairs={{16,32},{48,64},{80,96},{32,16},{64,48},{96,80},{17,33},{49,65},{8... | collective-permute-start | bytes 245768 | tf_op jit(solution)/shard_map/ppermute | solution.py:163
  20.0 10.8 %collective-permute-start.2 = (s32[8,8,256]{2,1,0:T(8,128)S(1)}, s32[8,8,256]{2,1,0:T(8,128)S(1)}, u32[]{:S(2)}, u32[]{:S(2)}) collective-permute-start(s32[8,8,256]{2,1,0:T(8,128)S(1)} %get-tuple-element.34), channel_id=1, source_target_pairs={{0,1},{2,3},{4,5},{6,7},{8,9},{10,11},{12,13},{14,15},{1,0},{3,2},... | collective-permute-start | bytes 196616 | tf_op jit(solution)/shard_map/ppermute | solution.py:163
  21.0 11.4 %copy-start.2 = (s32[1,128]{1,0:T(1,128)S(1)}, s32[1,128]{1,0:T(1,128)}, u32[]{:S(2)}) copy-start(s32[1,128]{1,0:T(1,128)} %owner.1) | copy-start | bytes 1540
  21.0 9.8 %collective-permute-start.3 = (s32[8,8,256]{2,1,0:T(8,128)S(1)}, s32[8,8,256]{2,1,0:T(8,128)S(1)}, u32[]{:S(2)}, u32[]{:S(2)}) collective-permute-start(s32[8,8,256]{2,1,0:T(8,128)S(1)} %get-tuple-element.35), channel_id=1, source_target_pairs={{1,2},{3,4},{5,6},{7,8},{9,10},{11,12},{13,14},{2,1},{4,3},{6,5},{... | collective-permute-start | bytes 196616 | tf_op jit(solution)/shard_map/ppermute | solution.py:163
  38.2 13.6 %collective-permute-start.4 = (bf16[5,32,256]{2,1,0:T(8,128)(2,1)S(1)}, bf16[5,32,256]{2,1,0:T(8,128)(2,1)S(1)}, u32[]{:S(2)}, u32[]{:S(2)}) collective-permute-start(bf16[5,32,256]{2,1,0:T(8,128)(2,1)S(1)} %get-tuple-element.39), channel_id=1, source_target_pairs={{0,16},{32,48},{64,80},{96,112},{16,0},{48,32},{80,64},{112,96},{1... | collective-permute-start | bytes 245768 | tf_op jit(solution)/shard_map/ppermute | solution.py:163
  40.7 11.2 %collective-permute-start.5 = (bf16[5,32,256]{2,1,0:T(8,128)(2,1)S(1)}, bf16[5,32,256]{2,1,0:T(8,128)(2,1)S(1)}, u32[]{:S(2)}, u32[]{:S(2)}) collective-permute-start(bf16[5,32,256]{2,1,0:T(8,128)(2,1)S(1)} %get-tuple-element.40), channel_id=1, source_target_pairs={{16,32},{48,64},{80,96},{32,16},{64,48},{96,80},{17,33},{49,65},{8... | collective-permute-start | bytes 245768 | tf_op jit(solution)/shard_map/ppermute | solution.py:163
  42.6 5.1 %collective-permute-start.6 = (bf16[8,16,256]{2,1,0:T(8,128)(2,1)S(1)}, bf16[8,16,256]{2,1,0:T(8,128)(2,1)S(1)}, u32[]{:S(2)}, u32[]{:S(2)}) collective-permute-start(bf16[8,16,256]{2,1,0:T(8,128)(2,1)S(1)} %get-tuple-element.41), channel_id=1, source_target_pairs={{0,1},{2,3},{4,5},{6,7},{8,9},{10,11},{12,13},{14,15},{1,0},{3,2},... | collective-permute-start | bytes 196616 | tf_op jit(solution)/shard_map/ppermute | solution.py:163
  44.1 7.7 %collective-permute-start.7 = (bf16[8,16,256]{2,1,0:T(8,128)(2,1)S(1)}, bf16[8,16,256]{2,1,0:T(8,128)(2,1)S(1)}, u32[]{:S(2)}, u32[]{:S(2)}) collective-permute-start(bf16[8,16,256]{2,1,0:T(8,128)(2,1)S(1)} %get-tuple-element.42), channel_id=1, source_target_pairs={{1,2},{3,4},{5,6},{7,8},{9,10},{11,12},{13,14},{2,1},{4,3},{6,5},{... | collective-permute-start | bytes 196616 | tf_op jit(solution)/shard_map/ppermute | solution.py:163
  55.6 13.0 %collective-permute-start.8 = (bf16[5,32,256]{2,1,0:T(8,128)(2,1)S(1)}, bf16[5,32,256]{2,1,0:T(8,128)(2,1)S(1)}, u32[]{:S(2)}, u32[]{:S(2)}) collective-permute-start(bf16[5,32,256]{2,1,0:T(8,128)(2,1)S(1)} %get-tuple-element.44), channel_id=1, source_target_pairs={{0,16},{32,48},{64,80},{96,112},{16,0},{48,32},{80,64},{112,96},{1... | collective-permute-start | bytes 245768 | tf_op jit(solution)/shard_map/ppermute | solution.py:163
  58.9 9.8 %collective-permute-start.9 = (bf16[5,32,256]{2,1,0:T(8,128)(2,1)S(1)}, bf16[5,32,256]{2,1,0:T(8,128)(2,1)S(1)}, u32[]{:S(2)}, u32[]{:S(2)}) collective-permute-start(bf16[5,32,256]{2,1,0:T(8,128)(2,1)S(1)} %get-tuple-element.45), channel_id=1, source_target_pairs={{16,32},{48,64},{80,96},{32,16},{64,48},{96,80},{17,33},{49,65},{8... | collective-permute-start | bytes 245768 | tf_op jit(solution)/shard_map/ppermute | solution.py:163
  60.8 4.6 %collective-permute-start.10 = (bf16[8,16,256]{2,1,0:T(8,128)(2,1)S(1)}, bf16[8,16,256]{2,1,0:T(8,128)(2,1)S(1)}, u32[]{:S(2)}, u32[]{:S(2)}) collective-permute-start(bf16[8,16,256]{2,1,0:T(8,128)(2,1)S(1)} %get-tuple-element.46), channel_id=1, source_target_pairs={{0,1},{2,3},{4,5},{6,7},{8,9},{10,11},{12,13},{14,15},{1,0},{3,2},... | collective-permute-start | bytes 196616 | tf_op jit(solution)/shard_map/ppermute | solution.py:163
  60.9 7.7 %collective-permute-start.11 = (bf16[8,16,256]{2,1,0:T(8,128)(2,1)S(1)}, bf16[8,16,256]{2,1,0:T(8,128)(2,1)S(1)}, u32[]{:S(2)}, u32[]{:S(2)}) collective-permute-start(bf16[8,16,256]{2,1,0:T(8,128)(2,1)S(1)} %get-tuple-element.47), channel_id=1, source_target_pairs={{1,2},{3,4},{5,6},{7,8},{9,10},{11,12},{13,14},{2,1},{4,3},{6,5},{... | collective-permute-start | bytes 196616 | tf_op jit(solution)/shard_map/ppermute | solution.py:163
  72.4 13.6 %collective-permute-start.12 = (bf16[5,32,256]{2,1,0:T(8,128)(2,1)S(1)}, bf16[5,32,256]{2,1,0:T(8,128)(2,1)S(1)}, u32[]{:S(2)}, u32[]{:S(2)}) collective-permute-start(bf16[5,32,256]{2,1,0:T(8,128)(2,1)S(1)} %get-tuple-element.49), channel_id=1, source_target_pairs={{0,16},{32,48},{64,80},{96,112},{16,0},{48,32},{80,64},{112,96},{1... | collective-permute-start | bytes 245768 | tf_op jit(solution)/shard_map/ppermute | solution.py:163
  74.7 11.3 %collective-permute-start.13 = (bf16[5,32,256]{2,1,0:T(8,128)(2,1)S(1)}, bf16[5,32,256]{2,1,0:T(8,128)(2,1)S(1)}, u32[]{:S(2)}, u32[]{:S(2)}) collective-permute-start(bf16[5,32,256]{2,1,0:T(8,128)(2,1)S(1)} %get-tuple-element.50), channel_id=1, source_target_pairs={{16,32},{48,64},{80,96},{32,16},{64,48},{96,80},{17,33},{49,65},{8... | collective-permute-start | bytes 245768 | tf_op jit(solution)/shard_map/ppermute | solution.py:163
  78.2 5.2 %collective-permute-start.14 = (bf16[8,16,256]{2,1,0:T(8,128)(2,1)S(1)}, bf16[8,16,256]{2,1,0:T(8,128)(2,1)S(1)}, u32[]{:S(2)}, u32[]{:S(2)}) collective-permute-start(bf16[8,16,256]{2,1,0:T(8,128)(2,1)S(1)} %get-tuple-element.51), channel_id=1, source_target_pairs={{0,1},{2,3},{4,5},{6,7},{8,9},{10,11},{12,13},{14,15},{1,0},{3,2},... | collective-permute-start | bytes 196616 | tf_op jit(solution)/shard_map/ppermute | solution.py:163
  78.3 7.7 %collective-permute-start.15 = (bf16[8,16,256]{2,1,0:T(8,128)(2,1)S(1)}, bf16[8,16,256]{2,1,0:T(8,128)(2,1)S(1)}, u32[]{:S(2)}, u32[]{:S(2)}) collective-permute-start(bf16[8,16,256]{2,1,0:T(8,128)(2,1)S(1)} %get-tuple-element.52), channel_id=1, source_target_pairs={{1,2},{3,4},{5,6},{7,8},{9,10},{11,12},{13,14},{2,1},{4,3},{6,5},{... | collective-permute-start | bytes 196616 | tf_op jit(solution)/shard_map/ppermute | solution.py:163

commit v3 on v2

--- a/solution.py
+++ b/solution.py
@@ -27,7 +27,7 @@
     return pltpu.with_memory_space_constraint(array, space)
 
 
-def call(body, outs, args, scratch=(), name=None, smem=(), hbm=(), hbm_outs=(), limit=24 * MIB, cost=4 * MIB):
+def call(body, outs, args, scratch=(), smem=(), hbm=(), hbm_outs=(), aliases=None, limit=24 * MIB, cost=4 * MIB):
     space = lambda i: pltpu.SMEM if i in smem else pltpu.HBM if i in hbm else pltpu.VMEM
     out_space = lambda i: pltpu.HBM if i in hbm_outs else pltpu.VMEM
     return pl.pallas_call(
@@ -36,9 +36,9 @@
         in_specs=[pl.BlockSpec(memory_space=space(i)) for i in range(len(args))],
         out_specs=[pl.BlockSpec(memory_space=out_space(i)) for i in range(len(outs))],
         scratch_shapes=list(scratch),
+        input_output_aliases=aliases or {},
         compiler_params=pltpu.CompilerParams(vmem_limit_bytes=limit),
         cost_estimate=pl.CostEstimate(flops=cost * 8, bytes_accessed=cost, transcendentals=0),
-        name=name,
     )(*[a if i in smem else in_space(a, space(i)) for i, a in enumerate(args)])
 
 
@@ -60,7 +60,7 @@
 
 SPAN_FACE = ((NCONS, CC, CN), BF16)
 CHORD_FACE = ((CS // 2, 16, CN), BF16)
-FACES = [SPAN_FACE, SPAN_FACE, CHORD_FACE, CHORD_FACE]
+FACES = [CHORD_FACE, CHORD_FACE, SPAN_FACE, SPAN_FACE]
 SPAN_HALO = pltpu.VMEM((2, NCONS, CC, CN), F32)
 CHORD_HALO = pltpu.VMEM((2, CS, 8, CN), F32)
 
@@ -69,23 +69,25 @@
     return lax.rem(lax.axis_index(axis), 2)
 
 
-def unpack_faces(faces, span_halo, chord_halo):
-    span_a, span_b, chord_a, chord_b = faces
+def unpack_span(faces, span_halo):
     p = parity("span")
-    for face, side in ((span_a, 1 - p), (span_b, p)):
+    for face, side in zip(faces, (1 - p, p)):
         for m in range(NCONS):
             for pair in range(CC // 16):
                 span_halo[side, m, wide_rows(pair), :] = face[m, wide_rows(pair), :].astype(F32)
+
+
+def unpack_chord(faces, chord_halo, groups=range(CS // 2)):
     p = parity("chord")
-    for face, side in ((chord_a, 1 - p), (chord_b, p)):
-        for group in range(CS // 2):
+    for face, side in zip(faces, (1 - p, p)):
+        for group in groups:
             both = face[group].astype(F32)
             chord_halo[side, 2 * group] = both[:8]
             chord_halo[side, 2 * group + 1] = both[8:]
 
 
 def pack_faces(cells, chord_edge, faces):
-    span_a, span_b, chord_a, chord_b = faces
+    chord_b, chord_a, span_b, span_a = faces
     p = parity("span")
     for face, side in ((span_a, 1 - p), (span_b, p)):
         for m in range(NCONS):
@@ -109,11 +111,11 @@
 
 START_SPAN = ((NCONS, CC // 2, CN), jnp.int32)
 START_CHORD = ((CS // 2, 8, CN), jnp.int32)
-START_FACES = [START_SPAN, START_SPAN, START_CHORD, START_CHORD]
+START_FACES = [START_CHORD, START_CHORD, START_SPAN, START_SPAN]
 
 
 def pack_start(cells, chord_edge, faces):
-    span_a, span_b, chord_a, chord_b = faces
+    chord_b, chord_a, span_b, span_a = faces
     p = parity("span")
     for face, side in ((span_a, 1 - p), (span_b, p)):
         for m in range(NCONS):
@@ -127,7 +129,7 @@
 
 
 def unpack_start(faces, span_halo, chord_halo):
-    span_a, span_b, chord_a, chord_b = faces
+    chord_b, chord_a, span_b, span_a = faces
     p = parity("span")
     for face, side in ((span_a, 1 - p), (span_b, p)):
         for m in range(NCONS):
@@ -147,13 +149,13 @@
             chord_edge[side, s] = jnp.zeros((8, CN), F32)
 
 
-def faces_body(cells, span_a, span_b, chord_a, chord_b, chord_edge):
+def faces_body(cells, chord_b, chord_a, span_b, span_a, chord_edge):
     clear_padding(chord_edge)
     for s in range(CS):
         for m in range(NCONS):
             chord_edge[0, s, pl.ds(m, 1), :] = cells[m, s, pl.ds(0, 1), :]
             chord_edge[1, s, pl.ds(m, 1), :] = cells[m, s, pl.ds(CC - 1, 1), :]
-    pack_start(cells, chord_edge, (span_a, span_b, chord_a, chord_b))
+    pack_start(cells, chord_edge, (chord_b, chord_a, span_b, span_a))
 
 
 def exchange(faces):
@@ -162,12 +164,8 @@
         pairs = [(i, i + 1) for i in range(start, count - 1, 2)]
         return lax.ppermute(face, axis, pairs + [(b, a) for a, b in pairs])
 
-    span_a, span_b, chord_a, chord_b = faces
-    span_b = swap(span_b, "span", 1)
-    span_a = swap(span_a, "span", 0)
-    chord_b = swap(chord_b, "chord", 1)
-    chord_a = swap(chord_a, "chord", 0)
-    return span_a, span_b, chord_a, chord_b
+    chord_b, chord_a, span_b, span_a = faces
+    return swap(chord_b, "chord", 1), swap(chord_a, "chord", 0), swap(span_b, "span", 1), swap(span_a, "span", 0)
 
 
 class Field:
@@ -232,14 +230,17 @@
     return out
 
 
-def each_row(row):
-    row(0, -1)
-
+def inner_rows(row):
     def inner(s, carry):
         row(s, 0)
         return carry
 
     lax.fori_loop(1, CS - 1, inner, 0)
+
+
+def each_row(row):
+    row(0, -1)
+    inner_rows(row)
     row(CS - 1, 1)
 
 
@@ -318,7 +319,6 @@
         smem=(1,),
         hbm=(0,),
         hbm_outs=(0,),
-        name="send_order",
         cost=3 * MIB,
     )[0]
 
@@ -443,39 +443,58 @@
         put(out, stencil(field, s, t, edge, factors, energies, base, coupling), s, t, chord_edge)
 
 
-def sweep_body(v, factor, scaled, coupling, fa, fb, fc, fd, out, ga, gb, gc, gd, span_halo, chord_halo, chord_edge):
-    unpack_faces((fa, fb, fc, fd), span_halo, chord_halo)
+def inner_body(v, factor, scaled, coupling, fc, fd, out, chord_edge, chord_halo):
+    unpack_chord((fc, fd), chord_halo)
     clear_padding(chord_edge)
+    field = Field(v, None, chord_halo)
+    inner_rows(lambda s, edge: sweep_row(field, factor, scaled, coupling, out, chord_edge, s, edge))
+
+
+def ends_body(v, factor, scaled, coupling, fc, fd, fa, fb, before, before_edge, out, chord_edge, ga, gb, gc, gd, span_halo, chord_halo):
+    unpack_chord((fc, fd), chord_halo, (0, CS // 2 - 1))
+    unpack_span((fa, fb), span_halo)
     field = Field(v, span_halo, chord_halo)
-    each_row(lambda s, edge: sweep_row(field, factor, scaled, coupling, out, chord_edge, s, edge))
+    for s, edge in ((0, -1), (CS - 1, 1)):
+        sweep_row(field, factor, scaled, coupling, out, chord_edge, s, edge)
     pack_faces(out, chord_edge, (ga, gb, gc, gd))
 
 
-def last_body(v, factor, scaled, coupling, fa, fb, fc, fd, out, cells, span_halo, chord_halo, out_sem):
-    unpack_faces((fa, fb, fc, fd), span_halo, chord_halo)
+def last_inner_body(v, factor, scaled, coupling, fc, fd, out, cells, chord_halo, out_sem):
+    unpack_chord((fc, fd), chord_halo)
+    field = Field(v, None, chord_halo)
+    put_out = lambda s: pltpu.make_async_copy(cells.at[:, s], out.at[:, s], out_sem.at[s])
+
+    def row(s, edge):
+        sweep_row(field, factor, scaled, coupling, cells, None, s, edge)
+        put_out(s).start()
+
+    inner_rows(row)
+    for s in range(1, CS - 1):
+        put_out(s).wait()
+
+
+def last_ends_body(v, factor, scaled, coupling, fc, fd, fa, fb, before, out, cells, span_halo, chord_halo, out_sem):
+    unpack_chord((fc, fd), chord_halo, (0, CS // 2 - 1))
+    unpack_span((fa, fb), span_halo)
     field = Field(v, span_halo, chord_halo)
     put_out = lambda s: pltpu.make_async_copy(cells.at[:, s], out.at[:, s], out_sem.at[s])
-
-    def row(s, edge):
+    for s, edge in ((0, -1), (CS - 1, 1)):
         sweep_row(field, factor, scaled, coupling, cells, None, s, edge)
-        if edge >= 0:
-            put_out(s - 1).start()
-
-    each_row(row)
-    put_out(CS - 1).start()
-    for s in range(CS):
+        put_out(s).start()
+    for s in (0, CS - 1):
         put_out(s).wait()
 
 
 BLOCK = (NCONS, CS, CC, CN)
 CELLS = (BLOCK, F32)
+EDGES = ((2, CS, 8, CN), F32)
 ROW_SEMS = pltpu.SemaphoreType.DMA((CS,))
 
 
 def shards(adjoint_next, objective_grad, state_next, checkpoint_pieces, slot_target, piece_owner, coupling):
     outgoing = send_order(checkpoint_pieces, slot_target)
     incoming = lax.all_to_all(outgoing, ("span", "chord"), split_axis=0, concat_axis=0, tiled=True)
-    halo = exchange(call(faces_body, START_FACES, [adjoint_next], scratch=[CHORD_HALO], name="faces", cost=MIB // 2))
+    halo = exchange(call(faces_body, START_FACES, [adjoint_next], scratch=[CHORD_HALO], cost=MIB // 2))
     right, span_next, chord_next = call(
         right_body,
         [CELLS, ((2, CC, CN), F32), ((2, CS, 8, CN), F32)],
@@ -490,7 +509,6 @@
         smem=(3,),
         hbm=(1, 2),
         hbm_outs=(0,),
-        name="right_side",
         cost=9 * MIB,
     )
     adjoint, factor, scaled, *faces = call(
@@ -508,29 +526,43 @@
         ],
         smem=(2, 4),
         hbm=(1, 3),
-        name="first_sweep",
         cost=9 * MIB,
     )
-    for sweep in range(2, SWEEPS):
-        adjoint, *faces = call(
-            sweep_body,
-            [CELLS, *FACES],
-            [adjoint, factor, scaled, coupling, *exchange(faces)],
-            scratch=[SPAN_HALO, CHORD_HALO, CHORD_HALO],
+    for sweep in range(2, SWEEPS + 1):
+        last = sweep == SWEEPS
+        chord_b, chord_a, span_b, span_a = exchange(faces)
+        known = [adjoint, factor, scaled, coupling, chord_a, chord_b]
+        if last:
+            inner = call(
+                last_inner_body,
+                [CELLS],
+                known,
+                scratch=[pltpu.VMEM(BLOCK, F32), CHORD_HALO, ROW_SEMS],
+                smem=(3,),
+                hbm_outs=(0,),
+                cost=8 * MIB,
+            )
+            return call(
+                last_ends_body,
+                [CELLS],
+                [*known, span_a, span_b, *inner],
+                scratch=[pltpu.VMEM(BLOCK, F32), SPAN_HALO, CHORD_HALO, ROW_SEMS],
+                smem=(3,),
+                hbm=(8,),
+                hbm_outs=(0,),
+                aliases={8: 0},
+                cost=MIB,
+            )[0]
+        inner = call(inner_body, [CELLS, EDGES], known, scratch=[CHORD_HALO], smem=(3,), cost=8 * MIB)
+        adjoint, _, *faces = call(
+            ends_body,
+            [CELLS, EDGES, *FACES],
+            [*known, span_a, span_b, *inner],
+            scratch=[SPAN_HALO, CHORD_HALO],
             smem=(3,),
-            name="sweep",
-            cost=9 * MIB,
+            aliases={8: 0, 9: 1},
+            cost=MIB,
         )
-    return call(
-        last_body,
-        [CELLS],
-        [adjoint, factor, scaled, coupling, *exchange(faces)],
-        scratch=[pltpu.VMEM(BLOCK, F32), SPAN_HALO, CHORD_HALO, ROW_SEMS],
-        smem=(3,),
-        hbm_outs=(0,),
-        name="last_sweep",
-        cost=9 * MIB,
-    )[0]
 
 
 def solution(mesh):

time: 92.5 us -> 95.8 us (1.036)
  the two profiles are of different devices: /device:TPU:39 before, /device:TPU:24 now
where the time goes in v3:
time: 95.8 us; the launch traced here: 95.4 us
  starting transfers between devices  49.1 us (51%)
  Pallas kernels  30.8 us (32%)
  waiting for transfers between devices  14.3 us (15%)
    ppermute x16, starting transfers between devices, swap(): return lax.ppermute(face, axis, pairs + [(b, a) for a, b in pairs])  38.4 us
    pallas_call x10, Pallas kernels, call(): pl.pallas_call(body, out_shape=[out_space(i)(shape, dtype) for i, (shape,...  30.8 us
    ppermute x16, waiting for transfers between devices, swap(): return lax.ppermute(face, axis, pairs + [(b, a) for a, b in pairs])  12.9 us
    all_to_all x1, starting transfers between devices, shards(): lax.all_to_all(outgoing, ('span', 'chord'), split_axis=0, concat_axis=0,...  10.7 us
  transfers between devices with their start and end apart: 17, of which 5 were waited for; matrix products, arithmetic and copies ran while one was open for 0% of the time, Pallas kernels for 18%

profile of v3, /device:TPU:24, one launch (start us, length us, event | category | flops | bytes accessed | tf_op | source)
XLA Modules:
  0.0 95.4 jit_solution(10180470456885801984)
XLA Ops:
  0.0 0.8 copy-done.3
  0.8 3.2 %shard_map.73 = s32[128,2,8,128]{3,2,1,0:T(8,128)} custom-call(bf16[8,128,1024]{2,1,0:T(8,128)(2,1)} %pieces.1, s32[1,128]{1,0:T(1,128)S(1)} %copy-done.3), custom_call_target="tpu_custom_call" | custom-call | flops 25165824 | bytes 3145728 | tf_op jit(solution)/shard_map/pallas_call | solution.py:33
  4.0 10.7 %all-to-all-start = ((s32[128,2,8,128]{3,2,1,0:T(8,128)}), s32[128,2,8,128]{3,2,1,0:T(8,128)}, u32[]{:S(2)}, u32[]{:S(2)}) async-start(s32[128,2,8,128]{3,2,1,0:T(8,128)} %shard_map.73), calls=%async_computation | async-start | bytes 2097152 | tf_op jit(solution)/shard_map/all_to_all | solution.py:496
  14.9 4.4 %collective-permute-start.2 = (s32[5,16,256]{2,1,0:T(8,128)S(1)}, s32[5,16,256]{2,1,0:T(8,128)S(1)}, u32[]{:S(2)}, u32[]{:S(2)}) collective-permute-start(s32[5,16,256]{2,1,0:T(8,128)S(1)} %get-tuple-element.38), channel_id=1, source_target_pairs={{16,32},{48,64},{80,96},{32,16},{64,48},{96,80},{17,33},{49,65},{8... | collective-permute-start | bytes 245768 | tf_op jit(solution)/shard_map/ppermute | solution.py:165
  19.4 3.4 %collective-permute-start = (s32[8,8,256]{2,1,0:T(8,128)S(1)}, s32[8,8,256]{2,1,0:T(8,128)S(1)}, u32[]{:S(2)}, u32[]{:S(2)}) collective-permute-start(s32[8,8,256]{2,1,0:T(8,128)S(1)} %get-tuple-element.36), channel_id=1, source_target_pairs={{1,2},{3,4},{5,6},{7,8},{9,10},{11,12},{13,14},{2,1},{4,3},{6,5},{... | collective-permute-start | bytes 196616 | tf_op jit(solution)/shard_map/ppermute | solution.py:165
  23.0 6.8 %shard_map.74 = (f32[5,16,32,256]{3,2,1,0:T(8,128)}, f32[2,32,256]{2,1,0:T(8,128)S(1)}, f32[2,16,8,256]{3,2,1,0:T(8,128)S(1)}) custom-call(f32[5,16,32,256]{3,2,1,0:T(8,128)S(1)} %copy-done, bf16[8,16,32,256]{3,2,1,0:T(8,128)(2,1)} %state.1, bf16[5,16,32,256]{3,2,1,0:T(8,128)(2,1)} %grad.1, f32[5,5]{1,0:T(8,128)S(1)} %copy-done.1), custom_call_target="tpu_custom_call" | custom-call | flops 75497472 | bytes 9437184 | tf_op jit(solution)/shard_map/pallas_call | solution.py:33
  30.5 1.4 %all-to-all-done.words = s32[128,2,8,128]{3,2,1,0:T(8,128)} async-done(((s32[128,2,8,128]{3,2,1,0:T(8,128)}), s32[128,2,8,128]{3,2,1,0:T(8,128)}, u32[]{:S(2)}, u32[]{:S(2)}) %all-to-all-start) | async-done | bytes 1048608 | tf_op jit(solution)/shard_map/all_to_all | solution.py:496
  32.0 6.1 %shard_map.76 = (f32[5,16,32,256]{3,2,1,0:T(8,128)S(1)}, f32[7,16,32,256]{3,2,1,0:T(8,128)S(1)}, f32[5,16,32,256]{3,2,1,0:T(8,128)S(1)}, bf16[8,16,256]{2,1,0:T(...) custom-call(f32[5,16,32,256]{3,2,1,0:T(8,128)S(1)} %copy-done, ...), custom_call_target="tpu_custom_call" | custom-call | flops 75497472 | bytes 9437184 | tf_op jit(solution)/shard_map/pallas_call | solution.py:33
  38.0 2.3 %collective-permute-start.6 = (bf16[5,32,256]{2,1,0:T(8,128)(2,1)S(1)}, bf16[5,32,256]{2,1,0:T(8,128)(2,1)S(1)}, u32[]{:S(2)}, u32[]{:S(2)}) collective-permute-start(bf16[5,32,256]{2,1,0:T(8,128)(2,1)S(1)} %get-tuple-element.45), channel_id=1, source_target_pairs={{0,16},{32,48},{64,80},{96,112},{16,0},{48,32},{80,64},{112,96},{1... | collective-permute-start | bytes 245768 | tf_op jit(solution)/shard_map/ppermute | solution.py:165
  40.3 3.7 %collective-permute-start.7 = (bf16[5,32,256]{2,1,0:T(8,128)(2,1)S(1)}, bf16[5,32,256]{2,1,0:T(8,128)(2,1)S(1)}, u32[]{:S(2)}, u32[]{:S(2)}) collective-permute-start(bf16[5,32,256]{2,1,0:T(8,128)(2,1)S(1)} %get-tuple-element.46), channel_id=1, source_target_pairs={{16,32},{48,64},{80,96},{32,16},{64,48},{96,80},{17,33},{49,65},{8... | collective-permute-start | bytes 245768 | tf_op jit(solution)/shard_map/ppermute | solution.py:165
  44.1 4.1 %collective-permute-start.5 = (bf16[8,16,256]{2,1,0:T(8,128)(2,1)S(1)}, bf16[8,16,256]{2,1,0:T(8,128)(2,1)S(1)}, u32[]{:S(2)}, u32[]{:S(2)}) collective-permute-start(bf16[8,16,256]{2,1,0:T(8,128)(2,1)S(1)} %get-tuple-element.44), channel_id=1, source_target_pairs={{1,2},{3,4},{5,6},{7,8},{9,10},{11,12},{13,14},{2,1},{4,3},{6,5},{... | collective-permute-start | bytes 196616 | tf_op jit(solution)/shard_map/ppermute | solution.py:165
  48.2 3.6 %collective-permute-done.5.fd = bf16[8,16,256]{2,1,0:T(8,128)(2,1)S(1)} collective-permute-done((bf16[8,16,256]{2,1,0:T(8,128)(2,1)S(1)}, bf16[8,16,256]{2,1,0:T(8,128)(2,1)S(1)}, u32[]{:S(2)}, u32[]{:S(2)}) %collective-permute-start.5) | collective-permute-done | bytes 65568 | tf_op jit(solution)/shard_map/ppermute | solution.py:165
  51.8 3.3 %shard_map.77 = (f32[5,16,32,256]{3,2,1,0:T(8,128)S(1)}, f32[2,16,8,256]{3,2,1,0:T(8,128)S(1)}) custom-call(f32[5,16,32,256]{3,2,1,0:T(8,128)S(1)} %get-tuple-element.40.v, f32[7,16,32,256]{3,2,1,0:T(8,128)S(1)} %get-tuple-element.41.factor, f32[5,16,32,256]{3,2,1,0:T(8,128)S(1)} %get-tuple-element.42.scaled, f32[5,5]{1,0:T(8,128)S(1)} %copy-done.1, ...), custom_call_target="tpu_custom_call" | custom-call | flops 67108864 | bytes 8388608 | tf_op jit(solution)/shard_map/pallas_call | solution.py:33
  55.1 1.1 %shard_map.78 = (f32[5,16,32,256]{3,2,1,0:T(8,128)S(1)}, f32[2,16,8,256]{3,2,1,0:T(8,128)S(1)}, bf16[8,16,256]{2,1,0:T(8,128)(2,1)S(1)}, bf16[8,16,256]{2,1,0:T(...) custom-call(f32[5,16,32,256]{3,2,1,0:T(8,128)S(1)} %get-tuple-elemen, ...), custom_call_target="tpu_custom_call", output_to_operand_aliasing={{0}: (8, {}), {1}: (9, {})} | custom-call | flops 8388608 | bytes 1048576 | tf_op jit(solution)/shard_map/pallas_call | solution.py:33
  56.3 6.6 %collective-permute-start.11 = (bf16[5,32,256]{2,1,0:T(8,128)(2,1)S(1)}, bf16[5,32,256]{2,1,0:T(8,128)(2,1)S(1)}, u32[]{:S(2)}, u32[]{:S(2)}) collective-permute-start(bf16[5,32,256]{2,1,0:T(8,128)(2,1)S(1)} %get-tuple-element.53), channel_id=1, source_target_pairs={{16,32},{48,64},{80,96},{32,16},{64,48},{96,80},{17,33},{49,65},{8... | collective-permute-start | bytes 245768 | tf_op jit(solution)/shard_map/ppermute | solution.py:165
  62.9 3.5 %collective-permute-start.9 = (bf16[8,16,256]{2,1,0:T(8,128)(2,1)S(1)}, bf16[8,16,256]{2,1,0:T(8,128)(2,1)S(1)}, u32[]{:S(2)}, u32[]{:S(2)}) collective-permute-start(bf16[8,16,256]{2,1,0:T(8,128)(2,1)S(1)} %get-tuple-element.51), channel_id=1, source_target_pairs={{1,2},{3,4},{5,6},{7,8},{9,10},{11,12},{13,14},{2,1},{4,3},{6,5},{... | collective-permute-start | bytes 196616 | tf_op jit(solution)/shard_map/ppermute | solution.py:165
  66.5 4.1 %collective-permute-done.9.fd = bf16[8,16,256]{2,1,0:T(8,128)(2,1)S(1)} collective-permute-done((bf16[8,16,256]{2,1,0:T(8,128)(2,1)S(1)}, bf16[8,16,256]{2,1,0:T(8,128)(2,1)S(1)}, u32[]{:S(2)}, u32[]{:S(2)}) %collective-permute-start.9) | collective-permute-done | bytes 65568 | tf_op jit(solution)/shard_map/ppermute | solution.py:165
  70.6 3.3 %shard_map.79 = (f32[5,16,32,256]{3,2,1,0:T(8,128)S(1)}, f32[2,16,8,256]{3,2,1,0:T(8,128)S(1)}) custom-call(f32[5,16,32,256]{3,2,1,0:T(8,128)S(1)} %get-tuple-element.49.v, f32[7,16,32,256]{3,2,1,0:T(8,128)S(1)} %get-tuple-element.41.factor, f32[5,16,32,256]{3,2,1,0:T(8,128)S(1)} %get-tuple-element.42.scaled, f32[5,5]{1,0:T(8,128)S(1)} %copy-done.1, ...), custom_call_target="tpu_custom_call" | custom-call | flops 67108864 | bytes 8388608 | tf_op jit(solution)/shard_map/pallas_call | solution.py:33
  73.9 1.1 %shard_map.80 = (f32[5,16,32,256]{3,2,1,0:T(8,128)S(1)}, f32[2,16,8,256]{3,2,1,0:T(8,128)S(1)}, bf16[8,16,256]{2,1,0:T(8,128)(2,1)S(1)}, bf16[8,16,256]{2,1,0:T(...) custom-call(f32[5,16,32,256]{3,2,1,0:T(8,128)S(1)} %get-tuple-elemen, ...), custom_call_target="tpu_custom_call", output_to_operand_aliasing={{0}: (8, {}), {1}: (9, {})} | custom-call | flops 8388608 | bytes 1048576 | tf_op jit(solution)/shard_map/pallas_call | solution.py:33
  75.1 6.6 %collective-permute-start.15 = (bf16[5,32,256]{2,1,0:T(8,128)(2,1)S(1)}, bf16[5,32,256]{2,1,0:T(8,128)(2,1)S(1)}, u32[]{:S(2)}, u32[]{:S(2)}) collective-permute-start(bf16[5,32,256]{2,1,0:T(8,128)(2,1)S(1)} %get-tuple-element.60), channel_id=1, source_target_pairs={{16,32},{48,64},{80,96},{32,16},{64,48},{96,80},{17,33},{49,65},{8... | collective-permute-start | bytes 245768 | tf_op jit(solution)/shard_map/ppermute | solution.py:165
  81.8 3.1 %collective-permute-start.13 = (bf16[8,16,256]{2,1,0:T(8,128)(2,1)S(1)}, bf16[8,16,256]{2,1,0:T(8,128)(2,1)S(1)}, u32[]{:S(2)}, u32[]{:S(2)}) collective-permute-start(bf16[8,16,256]{2,1,0:T(8,128)(2,1)S(1)} %get-tuple-element.58), channel_id=1, source_target_pairs={{1,2},{3,4},{5,6},{7,8},{9,10},{11,12},{13,14},{2,1},{4,3},{6,5},{... | collective-permute-start | bytes 196616 | tf_op jit(solution)/shard_map/ppermute | solution.py:165
  84.9 4.6 %collective-permute-done.13.fd = bf16[8,16,256]{2,1,0:T(8,128)(2,1)S(1)} collective-permute-done((bf16[8,16,256]{2,1,0:T(8,128)(2,1)S(1)}, bf16[8,16,256]{2,1,0:T(8,128)(2,1)S(1)}, u32[]{:S(2)}, u32[]{:S(2)}) %collective-permute-start.13) | collective-permute-done | bytes 65568 | tf_op jit(solution)/shard_map/ppermute | solution.py:165
  89.5 4.1 %shard_map.81.before = f32[5,16,32,256]{3,2,1,0:T(8,128)} custom-call(f32[5,16,32,256]{3,2,1,0:T(8,128)S(1)} %get-tuple-element.56.v, f32[7,16,32,256]{3,2,1,0:T(8,128)S(1)} %get-tuple-element.41.factor, f32[5,16,32,256]{3,2,1,0:T(8,128)S(1)} %get-tuple-element.42.scaled, f32[5,5]{1,0:T(8,128)S(1)} %copy-done.1, ...), custom_call_target="tpu_custom_call" | custom-call | flops 67108864 | bytes 8388608 | tf_op jit(solution)/shard_map/pallas_call | solution.py:33
  93.6 1.8 %shard_map.82 = f32[5,16,32,256]{3,2,1,0:T(8,128)} custom-call(f32[5,16,32,256]{3,2,1,0:T(8,128)S(1)} %get-tuple-element.56.v, f32[7,16,32,256]{3,2,1,0:T(8,128)S(1)} %get-tuple-element.41.factor, f32[5,16,32,256]{3,2,1,0:T(8,128)S(1)} %get-tuple-element.42.scaled, f32[5,5]{1,0:T(8,128)S(1)} %copy-done.1, ...), custom_call_target="tpu_custom_call", output_to_operand_aliasing={{}: (8, {})} | custom-call | flops 8388608 | bytes 1048576 | tf_op jit(solution)/shard_map/pallas_call | solution.py:33
  (28 shorter events, 1.5 us)
Async XLA Ops:
  0.0 14.8 %copy-start = (f32[5,16,32,256]{3,2,1,0:T(8,128)S(1)}, f32[5,16,32,256]{3,2,1,0:T(8,128)}, u32[]{:S(2)}) copy-start(f32[5,16,32,256]{3,2,1,0:T(8,128)} %v.3) | copy-start | bytes 7864324
  0.0 0.8 copy-start.3
  4.0 19.0 %copy-start.1 = (f32[5,5]{1,0:T(8,128)S(1)}, f32[5,5]{1,0:T(8,128)}, u32[]{:S(2)}) copy-start(f32[5,5]{1,0:T(8,128)} %coupling.15) | copy-start | bytes 304
  4.0 27.9 %all-to-all-start = ((s32[128,2,8,128]{3,2,1,0:T(8,128)}), s32[128,2,8,128]{3,2,1,0:T(8,128)}, u32[]{:S(2)}, u32[]{:S(2)}) async-start(s32[128,2,8,128]{3,2,1,0:T(8,128)} %shard_map.73), calls=%async_computation | async-start | bytes 2097152 | tf_op jit(solution)/shard_map/all_to_all | solution.py:496
  14.9 15.6 %collective-permute-start.2 = (s32[5,16,256]{2,1,0:T(8,128)S(1)}, s32[5,16,256]{2,1,0:T(8,128)S(1)}, u32[]{:S(2)}, u32[]{:S(2)}) collective-permute-start(s32[5,16,256]{2,1,0:T(8,128)S(1)} %get-tuple-element.38), channel_id=1, source_target_pairs={{16,32},{48,64},{80,96},{32,16},{64,48},{96,80},{17,33},{49,65},{8... | collective-permute-start | bytes 245768 | tf_op jit(solution)/shard_map/ppermute | solution.py:165
  19.3 11.2 %collective-permute-start.3 = (s32[5,16,256]{2,1,0:T(8,128)S(1)}, s32[5,16,256]{2,1,0:T(8,128)S(1)}, u32[]{:S(2)}, u32[]{:S(2)}) collective-permute-start(s32[5,16,256]{2,1,0:T(8,128)S(1)} %get-tuple-element.39), channel_id=1, source_target_pairs={{0,16},{32,48},{64,80},{96,112},{16,0},{48,32},{80,64},{112,96},{1... | collective-permute-start | bytes 245768 | tf_op jit(solution)/shard_map/ppermute | solution.py:165
  19.4 10.5 %collective-permute-start = (s32[8,8,256]{2,1,0:T(8,128)S(1)}, s32[8,8,256]{2,1,0:T(8,128)S(1)}, u32[]{:S(2)}, u32[]{:S(2)}) collective-permute-start(s32[8,8,256]{2,1,0:T(8,128)S(1)} %get-tuple-element.36), channel_id=1, source_target_pairs={{1,2},{3,4},{5,6},{7,8},{9,10},{11,12},{13,14},{2,1},{4,3},{6,5},{... | collective-permute-start | bytes 196616 | tf_op jit(solution)/shard_map/ppermute | solution.py:165
  22.9 9.1 %copy-start.2 = (s32[1,128]{1,0:T(1,128)S(1)}, s32[1,128]{1,0:T(1,128)}, u32[]{:S(2)}) copy-start(s32[1,128]{1,0:T(1,128)} %owner.1) | copy-start | bytes 1540
  22.9 7.0 %collective-permute-start.1 = (s32[8,8,256]{2,1,0:T(8,128)S(1)}, s32[8,8,256]{2,1,0:T(8,128)S(1)}, u32[]{:S(2)}, u32[]{:S(2)}) collective-permute-start(s32[8,8,256]{2,1,0:T(8,128)S(1)} %get-tuple-element.37), channel_id=1, source_target_pairs={{0,1},{2,3},{4,5},{6,7},{8,9},{10,11},{12,13},{14,15},{1,0},{3,2},... | collective-permute-start | bytes 196616 | tf_op jit(solution)/shard_map/ppermute | solution.py:165
  38.0 17.1 %collective-permute-start.6 = (bf16[5,32,256]{2,1,0:T(8,128)(2,1)S(1)}, bf16[5,32,256]{2,1,0:T(8,128)(2,1)S(1)}, u32[]{:S(2)}, u32[]{:S(2)}) collective-permute-start(bf16[5,32,256]{2,1,0:T(8,128)(2,1)S(1)} %get-tuple-element.45), channel_id=1, source_target_pairs={{0,16},{32,48},{64,80},{96,112},{16,0},{48,32},{80,64},{112,96},{1... | collective-permute-start | bytes 245768 | tf_op jit(solution)/shard_map/ppermute | solution.py:165
  40.3 14.8 %collective-permute-start.7 = (bf16[5,32,256]{2,1,0:T(8,128)(2,1)S(1)}, bf16[5,32,256]{2,1,0:T(8,128)(2,1)S(1)}, u32[]{:S(2)}, u32[]{:S(2)}) collective-permute-start(bf16[5,32,256]{2,1,0:T(8,128)(2,1)S(1)} %get-tuple-element.46), channel_id=1, source_target_pairs={{16,32},{48,64},{80,96},{32,16},{64,48},{96,80},{17,33},{49,65},{8... | collective-permute-start | bytes 245768 | tf_op jit(solution)/shard_map/ppermute | solution.py:165
  44.0 4.2 %collective-permute-start.4 = (bf16[8,16,256]{2,1,0:T(8,128)(2,1)S(1)}, bf16[8,16,256]{2,1,0:T(8,128)(2,1)S(1)}, u32[]{:S(2)}, u32[]{:S(2)}) collective-permute-start(bf16[8,16,256]{2,1,0:T(8,128)(2,1)S(1)} %get-tuple-element.43), channel_id=1, source_target_pairs={{0,1},{2,3},{4,5},{6,7},{8,9},{10,11},{12,13},{14,15},{1,0},{3,2},... | collective-permute-start | bytes 196616 | tf_op jit(solution)/shard_map/ppermute | solution.py:165
  44.1 7.7 %collective-permute-start.5 = (bf16[8,16,256]{2,1,0:T(8,128)(2,1)S(1)}, bf16[8,16,256]{2,1,0:T(8,128)(2,1)S(1)}, u32[]{:S(2)}, u32[]{:S(2)}) collective-permute-start(bf16[8,16,256]{2,1,0:T(8,128)(2,1)S(1)} %get-tuple-element.44), channel_id=1, source_target_pairs={{1,2},{3,4},{5,6},{7,8},{9,10},{11,12},{13,14},{2,1},{4,3},{6,5},{... | collective-permute-start | bytes 196616 | tf_op jit(solution)/shard_map/ppermute | solution.py:165
  56.2 17.8 %collective-permute-start.10 = (bf16[5,32,256]{2,1,0:T(8,128)(2,1)S(1)}, bf16[5,32,256]{2,1,0:T(8,128)(2,1)S(1)}, u32[]{:S(2)}, u32[]{:S(2)}) collective-permute-start(bf16[5,32,256]{2,1,0:T(8,128)(2,1)S(1)} %get-tuple-element.52), channel_id=1, source_target_pairs={{0,16},{32,48},{64,80},{96,112},{16,0},{48,32},{80,64},{112,96},{1... | collective-permute-start | bytes 245768 | tf_op jit(solution)/shard_map/ppermute | solution.py:165
  56.3 17.7 %collective-permute-start.11 = (bf16[5,32,256]{2,1,0:T(8,128)(2,1)S(1)}, bf16[5,32,256]{2,1,0:T(8,128)(2,1)S(1)}, u32[]{:S(2)}, u32[]{:S(2)}) collective-permute-start(bf16[5,32,256]{2,1,0:T(8,128)(2,1)S(1)} %get-tuple-element.53), channel_id=1, source_target_pairs={{16,32},{48,64},{80,96},{32,16},{64,48},{96,80},{17,33},{49,65},{8... | collective-permute-start | bytes 245768 | tf_op jit(solution)/shard_map/ppermute | solution.py:165
  62.8 3.6 %collective-permute-start.8 = (bf16[8,16,256]{2,1,0:T(8,128)(2,1)S(1)}, bf16[8,16,256]{2,1,0:T(8,128)(2,1)S(1)}, u32[]{:S(2)}, u32[]{:S(2)}) collective-permute-start(bf16[8,16,256]{2,1,0:T(8,128)(2,1)S(1)} %get-tuple-element.50), channel_id=1, source_target_pairs={{0,1},{2,3},{4,5},{6,7},{8,9},{10,11},{12,13},{14,15},{1,0},{3,2},... | collective-permute-start | bytes 196616 | tf_op jit(solution)/shard_map/ppermute | solution.py:165
  62.9 7.7 %collective-permute-start.9 = (bf16[8,16,256]{2,1,0:T(8,128)(2,1)S(1)}, bf16[8,16,256]{2,1,0:T(8,128)(2,1)S(1)}, u32[]{:S(2)}, u32[]{:S(2)}) collective-permute-start(bf16[8,16,256]{2,1,0:T(8,128)(2,1)S(1)} %get-tuple-element.51), channel_id=1, source_target_pairs={{1,2},{3,4},{5,6},{7,8},{9,10},{11,12},{13,14},{2,1},{4,3},{6,5},{... | collective-permute-start | bytes 196616 | tf_op jit(solution)/shard_map/ppermute | solution.py:165
  75.0 18.5 %collective-permute-start.14 = (bf16[5,32,256]{2,1,0:T(8,128)(2,1)S(1)}, bf16[5,32,256]{2,1,0:T(8,128)(2,1)S(1)}, u32[]{:S(2)}, u32[]{:S(2)}) collective-permute-start(bf16[5,32,256]{2,1,0:T(8,128)(2,1)S(1)} %get-tuple-element.59), channel_id=1, source_target_pairs={{0,16},{32,48},{64,80},{96,112},{16,0},{48,32},{80,64},{112,96},{1... | collective-permute-start | bytes 245768 | tf_op jit(solution)/shard_map/ppermute | solution.py:165
  75.1 18.5 %collective-permute-start.15 = (bf16[5,32,256]{2,1,0:T(8,128)(2,1)S(1)}, bf16[5,32,256]{2,1,0:T(8,128)(2,1)S(1)}, u32[]{:S(2)}, u32[]{:S(2)}) collective-permute-start(bf16[5,32,256]{2,1,0:T(8,128)(2,1)S(1)} %get-tuple-element.60), channel_id=1, source_target_pairs={{16,32},{48,64},{80,96},{32,16},{64,48},{96,80},{17,33},{49,65},{8... | collective-permute-start | bytes 245768 | tf_op jit(solution)/shard_map/ppermute | solution.py:165
  81.7 3.2 %collective-permute-start.12 = (bf16[8,16,256]{2,1,0:T(8,128)(2,1)S(1)}, bf16[8,16,256]{2,1,0:T(8,128)(2,1)S(1)}, u32[]{:S(2)}, u32[]{:S(2)}) collective-permute-start(bf16[8,16,256]{2,1,0:T(8,128)(2,1)S(1)} %get-tuple-element.57), channel_id=1, source_target_pairs={{0,1},{2,3},{4,5},{6,7},{8,9},{10,11},{12,13},{14,15},{1,0},{3,2},... | collective-permute-start | bytes 196616 | tf_op jit(solution)/shard_map/ppermute | solution.py:165
  81.8 7.7 %collective-permute-start.13 = (bf16[8,16,256]{2,1,0:T(8,128)(2,1)S(1)}, bf16[8,16,256]{2,1,0:T(8,128)(2,1)S(1)}, u32[]{:S(2)}, u32[]{:S(2)}) collective-permute-start(bf16[8,16,256]{2,1,0:T(8,128)(2,1)S(1)} %get-tuple-element.58), channel_id=1, source_target_pairs={{1,2},{3,4},{5,6},{7,8},{9,10},{11,12},{13,14},{2,1},{4,3},{6,5},{... | collective-permute-start | bytes 196616 | tf_op jit(solution)/shard_map/ppermute | solution.py:165
